TPU v7x, 128 devices: a whole 4x4x4 slice. The times are simulated.
128 devices in a mesh: gx: 16 (over x, y), gy: 8 (over z, core).
Axes of the slice: x: 4, y: 4, z: 4, core: 2. Of those that a mesh axis runs over, the one named last changes fastest.
Arguments:
- near_null: float32 [768, 64, 2048], P('gx', 'gy')
- a_blocks: bfloat16 [768, 64, 4, 4096], P('gx', 'gy'), may hold values from -0.375 to 0.375
- inv_diag: float32 [768, 64, 64], P('gx', 'gy'), may hold values from 0.5 to 2
- root_map: int32 [768, 64], P('gx', 'gy'), may hold values from 0 to 49151, as said below
- neighbours: int32 [768, 64, 4], P('gx', 'gy'), may hold values from 0 to 49151, as said below
Outputs:
- prolong: float32 [768, 64, 2048], P('gx', 'gy')
Inputs may be any that keep to these rules, and one draw needn't show every extreme that they name: `root_map`: each element's root lies within 2 elements of it along both grid dimensions, and every root is its own root. `neighbours`: entry 0 of each element's list is the element itself; the other 3 entries are distinct other elements within 2 elements of it along both grid dimensions.
All inputs are finite; a program needn't handle non-finite values.
Results may differ from a plain program's by a relative error of at most 0.0017.
Values may be sent and summed in bfloat16 or wider, within the bound.
A program may use at most 384 MiB of HBM per device.

v0:
```python
import functools

import jax
import jax.numpy as jnp
from jax import lax
from jax.experimental import pallas as pl
from jax.experimental.pallas import tpu as pltpu
from jax.sharding import PartitionSpec as P

F32 = jnp.float32
BF = jnp.bfloat16
OMEGA = 2.0 / 3.0

def pick_blocks(pieces, block):
    out = pieces[3]
    for b in (2, 1, 0):
        out = jnp.where(block == b, pieces[b], out)
    return out

def turn(v, s):
    s = s % 4
    return v if s == 0 else pltpu.roll(v, 32*s, 1)

def gram_kernel(xb, b_ref, g_ref, ybuf, zbuf, gbuf):
    block16 = lax.broadcasted_iota(jnp.int32, (16,128), 1)//32
    block32 = lax.broadcasted_iota(jnp.int32, (32,128), 1)//32
    block8 = lax.broadcasted_iota(jnp.int32, (8,128), 1)//32
    def one_x(xi, carry):
        for half in range(2):
            p = [b_ref[xi, pl.ds(4*half+b, 16, stride=8), :] for b in range(4)]
            for q in range(4):
                ybuf[half, pl.ds(q, 16, stride=4), :] = pick_blocks([turn(p[b], b-q) for b in range(4)], block16)
        for half in range(2):
            yh = ybuf[half].astype(BF)
            o = lax.dot_general(yh, yh, (((0,),(0,)),((),())), preferred_element_type=F32)
            zbuf[half] = pick_blocks([o[32*b:32*b+32] for b in range(4)], block32) * (1.0/64)
        for half in range(2):
            r = [zbuf[half, pl.ds(kq, 8, stride=4), :] for kq in range(4)]
            for b in range(4):
                gbuf[:, 4*half+b, :] = pick_blocks([turn(r[kq], kq-b) for kq in range(4)], block8)
        g_ref[:, xi] = gbuf[...].astype(BF)
        return carry
    lax.fori_loop(0, xb, one_x, 0)

def gram_call(nn, xb=12):
    nx = nn.shape[0]
    return pl.pallas_call(functools.partial(gram_kernel, xb), grid=(nx//xb,),
        in_specs=[pl.BlockSpec((xb,128,128), lambda i:(i,0,0))],
        out_specs=pl.BlockSpec((8,xb,8,128), lambda i:(0,i,0,0)),
        out_shape=jax.ShapeDtypeStruct((8,nx,8,128),BF),
        scratch_shapes=[pltpu.VMEM((2,64,128),F32), pltpu.VMEM((2,32,128),F32), pltpu.VMEM((8,8,128),F32)], name="gram")(nn)


def halo_kernel(nx, ny, width, xdim, ydim, with_tile, *refs):
    if with_tile:
        src, tile, dst, tiles, send, recv, own = refs
    else:
        src, dst, send, recv, own = refs
    gx, gy = lax.axis_index("gx"), lax.axis_index("gy")
    cx, cy = lax.axis_size("gx"), lax.axis_size("gy")
    sides = [(dx, dy) for dx in (-1, 0, 1) for dy in (-1, 0, 1) if dx or dy]

    def there(dx, dy):
        ok = jnp.bool_(True)
        if dx: ok &= (gx + dx >= 0) & (gx + dx < cx)
        if dy: ok &= (gy + dy >= 0) & (gy + dy < cy)
        return ok

    def taken(d, n):
        return pl.ds(0, n) if d == 0 else (pl.ds(n - width, width) if d > 0 else pl.ds(0, width))

    def landed(d, n):
        return pl.ds(width, n) if d == 0 else (pl.ds(0, width) if d > 0 else pl.ds(n + width, width))

    def view(ref, sx, sy):
        at = [slice(None)] * len(ref.shape)
        at[xdim], at[ydim] = sx, sy
        return ref.at[tuple(at)]

    def copies(s, dx, dy):
        to = (gx + dx, gy + dy)
        out = [pltpu.make_async_remote_copy(
            src_ref=view(src, taken(dx, nx), taken(dy, ny)), dst_ref=view(dst, landed(dx, nx), landed(dy, ny)),
            send_sem=send.at[0, s], recv_sem=recv.at[0, s], device_id=to, device_id_type=pl.DeviceIdType.MESH)]
        if with_tile:
            out.append(pltpu.make_async_remote_copy(
                src_ref=tile, dst_ref=tiles.at[1 - dx, 1 - dy],
                send_sem=send.at[1, s], recv_sem=recv.at[1, s], device_id=to, device_id_type=pl.DeviceIdType.MESH))
        return out

    barrier = pltpu.get_barrier_semaphore()
    for dx, dy in sides:
        @pl.when(there(dx, dy))
        def _():
            pl.semaphore_signal(barrier, inc=1, device_id=(gx + dx, gy + dy), device_id_type=pl.DeviceIdType.MESH)
    mine = [pltpu.make_async_copy(src, view(dst, pl.ds(width, nx), pl.ds(width, ny)), own.at[0])]
    if with_tile:
        mine.append(pltpu.make_async_copy(tile, tiles.at[1, 1], own.at[1]))
    for c in mine: c.start()
    wide = 1 + (gx > 0).astype(jnp.int32) + (gx < cx - 1).astype(jnp.int32)
    tall = 1 + (gy > 0).astype(jnp.int32) + (gy < cy - 1).astype(jnp.int32)
    pl.semaphore_wait(barrier, wide * tall - 1)
    for s, (dx, dy) in enumerate(sides):
        @pl.when(there(dx, dy))
        def _():
            for c in copies(s, dx, dy): c.start()
    for s, (dx, dy) in enumerate(sides):
        @pl.when(there(-dx, -dy))
        def _():
            for c in copies(s, dx, dy): c.wait_recv()
    for s, (dx, dy) in enumerate(sides):
        @pl.when(there(dx, dy))
        def _():
            for c in copies(s, dx, dy): c.wait_send()
    for c in mine: c.wait()


def halo_call(src, dst_shape, width, xdim, ydim, tile=None, collective_id=0, name="halo"):
    anyspec = pl.BlockSpec(memory_space=pl.ANY)
    outs = [jax.ShapeDtypeStruct(dst_shape, src.dtype)]
    args = [src]
    if tile is not None:
        outs.append(jax.ShapeDtypeStruct((3, 3) + tile.shape, tile.dtype))
        args.append(tile)
    n = len(args)
    return pl.pallas_call(functools.partial(halo_kernel, src.shape[xdim], src.shape[ydim], width, xdim, ydim, tile is not None),
        in_specs=[anyspec]*n, out_specs=[anyspec]*n, out_shape=outs,
        scratch_shapes=[pltpu.SemaphoreType.DMA((2,8)), pltpu.SemaphoreType.DMA((2,8)), pltpu.SemaphoreType.DMA((2,))],
        compiler_params=pltpu.CompilerParams(collective_id=collective_id, has_side_effects=True), name=name)(*args)


def factor_kernel(nx, cells_ref, slot_ref, edge_ref, rid_ref, b_ref, g_ref, t_ref, tb_ref, comp, idcol, tab, v_ref, g_buf, t16, sem):
    ncell = cells_ref.shape[0]
    px = nx + 8
    els = px * 16
    copy_g = pltpu.make_async_copy(g_ref, g_buf, sem)
    copy_g.start()
    def compact(i, n):
        cid = cells_ref[i]
        idcol[pl.ds(n, 1), :] = jnp.full((1, 128), cid, jnp.int32)
        comp[i] = n
        return n + (cid >= 0).astype(jnp.int32)
    n = lax.fori_loop(0, ncell, compact, 0, unroll=8)
    copy_g.wait()
    @pl.when(edge_ref[0] == 1)
    def _(): g_buf[:, 0:4] = jnp.zeros((8, 4, 16, 128), BF)
    @pl.when(edge_ref[1] == 1)
    def _(): g_buf[:, px-4:px] = jnp.zeros((8, 4, 16, 128), BF)
    sub16 = lax.broadcasted_iota(jnp.int32, (16, 128), 0)
    def clear(keep):
        def one(x, c):
            for k in range(8):
                g_buf[k, x] = jnp.where(keep, g_buf[k, x], jnp.zeros((16,128), BF))
            return c
        lax.fori_loop(0, px, one, 0)
    @pl.when(edge_ref[2] == 1)
    def _(): clear(sub16 >= 4)
    @pl.when(edge_ref[3] == 1)
    def _(): clear(sub16 < 12)

    sub = lax.broadcasted_iota(jnp.int32, (32, 128), 0)
    def batch(bi, c):
        base = bi*128
        ids = idcol[pl.ds(base, 128), :]
        hot = [jnp.where(ids == rid_ref[:, 128*t:128*t+128], 1.0, 0.0).astype(BF) for t in range(els//128)]
        hot = jnp.concatenate(hot, axis=1)
        for k4 in range(8):
            s = jnp.dot(hot, g_buf[k4].reshape(els, 128), preferred_element_type=F32)
            v_ref[128*k4:128*k4+128, :] = s.T
        for jb in range(4):
            def pivot(j8, c2):
                j = jb*8 + j8
                row = v_ref[pl.ds(pl.multiple_of(j*32, 32), 32), :]
                d = lax.rsqrt(v_ref[pl.ds(j*33, 1), :])
                at_j = sub == j
                u = jnp.where(at_j, d, row*d)
                v_ref[pl.ds(pl.multiple_of(j*32, 32), 32), :] = u
                keep = jnp.where(at_j, 0.0, 1.0)
                for i in range(jb*8, 32):
                    f = u[i:i+1, :]
                    old = v_ref[32*i:32*i+32, :]
                    if i < jb*8+8:
                        later = i > j
                        f = jnp.where(later, f, 0.0)
                        new = jnp.where(at_j & later, 0.0, old) - f*u
                        new = jnp.where(later, new, old)
                    else:
                        new = jnp.where(at_j, 0.0, old) - f*u
                    v_ref[32*i:32*i+32, :] = new
                return c2
            lax.fori_loop(0, 8, pivot, 0)
        for k in range(32):
            m = v_ref[pl.ds(k, 32, stride=32), :]
            m = jnp.where(sub >= k, m, 0.0)
            tab[k, pl.ds(base, 128), :] = jnp.concatenate([m]*4, axis=0).T
        return c
    lax.fori_loop(0, (n + 127)//128, batch, 0)

    block = lax.broadcasted_iota(jnp.int32, (32, 128), 1)//32
    def one_x(x, c):
        for y in range(8):
            r = comp[slot_ref[x*8+y]]
            w = tab[:, pl.ds(r, 1), :].reshape(32, 128)
            wh = w.astype(BF).astype(F32)
            wl = w - wh
            hi = jnp.concatenate([jnp.where(block == q, wh, 0.0) for q in range(4)], axis=0).astype(BF)
            lo = jnp.concatenate([jnp.where(block == q, wl, 0.0) for q in range(4)], axis=0).astype(BF)
            p = b_ref[x, pl.ds(y, 16, stride=8), :]
            ph = p.astype(BF)
            plo = (p - ph.astype(F32)).astype(BF)
            t = jnp.dot(ph, hi, preferred_element_type=F32) + jnp.dot(plo, hi, preferred_element_type=F32) + jnp.dot(ph, lo, preferred_element_type=F32)
            t_ref[x, pl.ds(y, 16, stride=8), :] = t
            tb_ref[x, y] = t.astype(BF)
        return c
    lax.fori_loop(0, nx, one_x, 0)

def factor_call(cells, slots, edge, rid, nn, gpad):
    nx = nn.shape[0]
    full = lambda s: pl.BlockSpec(s, lambda i,*_: (0,)*len(s), pipeline_mode=pl.Buffered(1))
    nc = (nx+4)*12
    ncp = (nc + 127)//128*128 + 128
    return pl.pallas_call(functools.partial(factor_kernel, nx),
        grid_spec=pltpu.PrefetchScalarGridSpec(num_scalar_prefetch=3, grid=(1,),
          in_specs=[full(rid.shape), full(nn.shape), pl.BlockSpec(memory_space=pl.ANY)],
          out_specs=[full(nn.shape), full((nx,8,16,128))],
          scratch_shapes=[pltpu.SMEM((nc,), jnp.int32), pltpu.VMEM((ncp,128), jnp.int32), pltpu.VMEM((32,ncp,128),F32), pltpu.VMEM((1024,128),F32), pltpu.VMEM(gpad.shape,BF), pltpu.VMEM((16,128),F32), pltpu.SemaphoreType.DMA]),
        out_shape=[jax.ShapeDtypeStruct(nn.shape,F32), jax.ShapeDtypeStruct((nx,8,16,128),BF)],
        compiler_params=pltpu.CompilerParams(vmem_limit_bytes=56<<20), name="factor")(cells, slots, edge, rid, nn, gpad)


def apply_kernel(nx, px, py, xb, idx_ref, t_ref, d_ref, sel_ref, tp_ref, a_ref, out_ref, abuf, table, wide, tall, scale_ref, sems):
    step = pl.program_id(0)
    steps = nx // xb
    def copies(s, slot):
        return [pltpu.make_async_copy(a_ref.at[pl.ds(s*xb, xb), :, :, pl.ds(2*kp, 2), :], abuf.at[slot, :, :, kp], sems.at[slot, kp]) for kp in range(2)]
    lane = lax.broadcasted_iota(jnp.int32, (16, 128), 1)
    @pl.when(step == 0)
    def _():
        for c in copies(0, 0): c.start()
        def expand(x, carry):
            rows = tp_ref[x].reshape(py*16, 128)
            o = jnp.dot(rows, sel_ref[...], preferred_element_type=F32)
            for y in range(py):
                for q in range(4):
                    tall[y, pl.ds(q, 16, stride=4), :] = o[y*16:(y+1)*16, q*128:(q+1)*128]
            for y in range(py):
                table[x*py+y] = tall[y].astype(BF)
            return carry
        lax.fori_loop(0, px, expand, 0)
    slot = lax.rem(step, 2)
    @pl.when(step + 1 < steps)
    def _():
        for c in copies(step+1, 1-slot): c.start()
    for c in copies(step, slot): c.wait()
    row8 = lax.broadcasted_iota(jnp.int32, (128, 64), 0) // 8
    col4 = lax.broadcasted_iota(jnp.int32, (128, 64), 1) // 4
    pick = (lax.broadcasted_iota(jnp.int32, (64, 128), 0) % 4 == lax.broadcasted_iota(jnp.int32, (64, 128), 1) // 32)
    pick = jnp.where(pick, 1.0, 0.0).astype(BF)
    lanew = lax.broadcasted_iota(jnp.int32, (64, 128), 1)
    def one_x(xi, carry):
        d = d_ref[xi] * OMEGA
        dt = jnp.where(row8 == col4, jnp.concatenate([d]*16, axis=0), 0.0)
        hi = dt.astype(BF); lo = (dt - hi.astype(F32)).astype(BF)
        scale_ref[...] = jnp.dot(hi, pick, preferred_element_type=F32) + jnp.dot(lo, pick, preferred_element_type=F32)
        for y in range(8):
            e4 = ((step*xb + xi)*8 + y)*4
            parts = []
            for kp in range(2):
                t0 = table[idx_ref[e4+2*kp]]
                t1 = table[idx_ref[e4+2*kp+1]]
                r = jnp.where(lanew < 64, t0, t1)
                parts.append(jnp.where((lanew//32) % 2 == 0, r, jnp.zeros_like(r)))
                parts.append(jnp.where((lanew//32) % 2 == 1, r, jnp.zeros_like(r)))
            rhs = jnp.concatenate(parts, axis=0)
            lhs = jnp.concatenate([abuf[slot, xi, y, 0].reshape(64,128), abuf[slot, xi, y, 1].reshape(64,128)], axis=1)
            wide[y] = jnp.dot(lhs, rhs, preferred_element_type=F32)
        for y in range(8):
            r = [wide[y, pl.ds(q, 16, stride=4), :] for q in range(4)]
            u = jnp.where(lane < 64, r[0], r[3]) + pltpu.roll(jnp.where(lane < 64, r[2], r[1]), 64, 1)
            rows = pl.ds(y, 16, stride=8)
            out_ref[xi, rows, :] = t_ref[xi, rows, :] - scale_ref[rows, :] * u
        return carry
    lax.fori_loop(0, xb, one_x, 0)

def spread_matrix():
    r = jnp.arange(128)[:, None]; c = jnp.arange(512)[None, :]
    return ((r//32 == c//128) & (r%32 == c%32)).astype(BF)

def apply_call(idx, t4, d, tp, a5, xb=4):
    nx = t4.shape[0]; px, py = tp.shape[:2]
    blk = pl.BlockSpec((xb,128,128), lambda i,*_:(i,0,0))
    return pl.pallas_call(functools.partial(apply_kernel, nx, px, py, xb),
        grid_spec=pltpu.PrefetchScalarGridSpec(num_scalar_prefetch=1, grid=(nx//xb,),
          in_specs=[blk, pl.BlockSpec((xb,8,64), lambda i,*_:(i,0,0)), pl.BlockSpec((128,512), lambda i,*_:(0,0)),
                    pl.BlockSpec((px,py,16,128), lambda i,*_:(0,0,0,0), pipeline_mode=pl.Buffered(1)), pl.BlockSpec(memory_space=pl.ANY)],
          out_specs=blk,
          scratch_shapes=[pltpu.VMEM((2,xb,8,2,32,2,128),BF), pltpu.VMEM((px*py,64,128),BF), pltpu.VMEM((8,64,128),F32), pltpu.VMEM((py,64,128),F32), pltpu.VMEM((128,128),F32), pltpu.SemaphoreType.DMA((2,2))]),
        out_shape=jax.ShapeDtypeStruct((nx,128,128),F32),
        compiler_params=pltpu.CompilerParams(vmem_limit_bytes=56<<20), name="apply")(idx, t4, d, spread_matrix(), tp, a5)


def body(near_null, a_blocks, inv_diag, root_map, neighbours):
    nx, ny = root_map.shape
    grid_x, grid_y = nx * lax.axis_size("gx"), ny * lax.axis_size("gy")
    gx, gy = lax.axis_index("gx"), lax.axis_index("gy")
    sx, sy = gx * nx, gy * ny
    nn = near_null.reshape(nx, ny, 16, 128).transpose(0, 2, 1, 3).reshape(nx, 128, 128)
    a5 = a_blocks.reshape(nx, ny, 4, 32, 128).transpose(0, 1, 3, 2, 4)
    tile = jnp.pad(root_map.T, ((0, 0), (0, 128 - nx)))
    grams = gram_call(nn)
    gpad, tiles = halo_call(grams, (8, nx + 8, ny + 8, 128), 4, 1, 2, tile=tile, collective_id=0, name="halo_gram")
    around = tiles[:, :, :, :nx].transpose(0, 3, 1, 2).reshape(3 * nx, 3 * ny)[nx - 4:2 * nx + 4, ny - 4:2 * ny + 4]
    ax = sx - 4 + jnp.arange(nx + 8, dtype=jnp.int32)[:, None]
    ay = sy - 4 + jnp.arange(ny + 8, dtype=jnp.int32)[None, :]
    around = jnp.where((ax >= 0) & (ax < grid_x) & (ay >= 0) & (ay < grid_y), around, -1)
    cells = jnp.where(around == ax * grid_y + ay, around, -1)[2:-2, 2:-2].reshape(-1)
    slots = ((root_map // grid_y - sx + 2) * (ny + 4) + root_map % grid_y - sy + 2).reshape(-1)
    edge = jnp.stack([gx == 0, gx == lax.axis_size("gx") - 1, gy == 0, gy == lax.axis_size("gy") - 1]).astype(jnp.int32)
    tent, low = factor_call(cells, slots, edge, around.reshape(1, -1), nn, gpad)
    (low_pad,) = halo_call(low, (nx + 4, ny + 4, 16, 128), 2, 0, 1, collective_id=1, name="halo_tent")
    idx = ((neighbours // grid_y - sx + 2) * (ny + 4) + neighbours % grid_y - sy + 2).reshape(-1)
    out = apply_call(idx, tent, inv_diag, low_pad, a5)
    return out.reshape(nx, 16, ny, 128).transpose(0, 2, 1, 3).reshape(nx, ny, 2048)


def solution(mesh):
    in_specs = (P("gx", "gy", None), P("gx", "gy", None, None), P("gx", "gy", None), P("gx", "gy"), P("gx", "gy", None))
    return jax.shard_map(body, mesh=mesh, in_specs=in_specs, out_specs=P("gx", "gy", None), check_vma=False)
```

profile of v0, /device:TPU:7, one launch (start us, length us, event | category | flops | bytes accessed | tf_op | source)
XLA Modules:
  0.0 169.4 jit_solution(10400118627449029953)
XLA Ops:
  0.0 0.7 add_convert_fusion.edge_ref
  0.7 0.1 slice.13
  0.7 0.1 slice.14
  0.8 1.3 pad.4.refs_1_
  2.1 0.7 fusion.13
  2.8 0.8 fusion.5
  3.6 0.1 copy.9
  3.7 0.7 reshape.164.slot_ref
  4.3 0.8 and_convert_fusion.sel_ref
  5.1 0.2 copy.6
  5.3 0.7 reshape.159.idx_ref
  6.0 22.7 %gram.1.refs_0_ = bf16[8,48,8,128]{3,2,1,0:T(8,128)(2,1)} custom-call(f32[48,128,128]{2,1,0:T(8,128)} %bitcast.23), custom_call_target="tpu_custom_call" | custom-call | tf_op jit(solution)/shard_map/gram/pallas_call | solution.py:47
  28.7 25.4 %halo_gram.1 = (bf16[8,56,16,128]{3,2,1,0:T(8,128)(2,1)}, s32[3,3,8,128]{3,2,1,0:T(8,128)}) custom-call(bf16[8,48,8,128]{3,2,1,0:T(8,128)(2,1)} %gram.1.refs_0_, s32[8,128]{1,0:T(8,128)} %pad.4.refs_1_), custom_call_target="tpu_custom_call" | custom-call | tf_op jit(solution)/shard_map/halo_gram/pallas_call | solution.py:126
  54.1 0.8 slice_bitcast_fusion
  54.9 0.1 reshape.162
  55.0 0.1 slice_select_fusion
  55.1 0.1 compare_select_fusion
  55.1 0.1 copy.10
  55.2 0.7 reshape.165.rid_ref
  55.9 0.1 copy.8
  56.0 0.7 reshape.163.cells_ref
  56.7 29.2 %factor.1 = (f32[48,128,128]{2,1,0:T(8,128)}, bf16[48,8,16,128]{3,2,1,0:T(8,128)(2,1)}) custom-call(s32[624]{0:T(1024)} %reshape.163.cells_ref, s32[384]{0:T(512)} %reshape.164.slot_ref, s32[4]{0:T(128)} %add_convert_fusion.edge_ref, s32[1,896]{1,0:T(1,128)} %reshape.165.rid_ref, f32[48,128,128]{2,1,0:T(8,128)} %bitcast.24, ...), custom_call_target="tpu_custom_call" | custom-call | tf_op jit(solution)/shard_map/factor/pallas_call | solution.py:222
  85.9 49.2 %halo_tent.1.tp_ref = bf16[52,12,16,128]{3,2,1,0:T(8,128)(2,1)} custom-call(bf16[48,8,16,128]{3,2,1,0:T(8,128)(2,1)} %get-tuple-element.12.refs_0_), custom_call_target="tpu_custom_call" | custom-call | tf_op jit(solution)/shard_map/halo_tent/pallas_call | solution.py:126
  135.2 34.3 %apply.1 = f32[48,128,128]{2,1,0:T(8,128)} custom-call(s32[1536]{0:T(1024)} %reshape.159.idx_ref, f32[48,128,128]{2,1,0:T(8,128)} %get-tuple-element.11.t_ref, f32[48,8,64]{2,1,0:T(8,128)} %d_ref.1, bf16[128,512]{1,0:T(8,128)(2,1)} %and_convert_fusion.sel_ref, bf16[52,12,16,128]{3,2,1,0:T(8,128)(2,1)} %halo_tent.1.tp_ref, bf16[48,8,32,4,128]{4,3,2,1,0:T(4,128)(2,1)} %bitcast.22), custom_call_target="tpu_custom_call" | custom-call | tf_op jit(solution)/shard_map/apply/pallas_call | solution.py:292
  (7 shorter events, 0.0 us)
where the time goes:
time: 171 us; the launch traced here: 169 us
  Pallas kernels  161 us (94%)
  local copies, waits for them, and re-layouts  5.48 us (3%)
  other arithmetic  3.06 us (2%)
    pallas_call x2, Pallas kernels, halo_call(): pl.pallas_call(functools.partial(halo_kernel, src.shape[xdim], src.shape[...  74.6 us
    pallas_call x1, Pallas kernels, apply_call(): pl.pallas_call(functools.partial(apply_kernel, nx, px, py, xb), grid_spec...  34.3 us
    pallas_call x1, Pallas kernels, factor_call(): pl.pallas_call(functools.partial(factor_kernel, nx), grid_spec=pltpu.Pref...  29.2 us
    pallas_call x1, Pallas kernels, gram_call(): pl.pallas_call(functools.partial(gram_kernel, xb), grid=(nx // xb,), in_s...  22.7 us

commit v1 on v0

v1 whole, which is shorter than its diff:
```python
import functools

import jax
import jax.numpy as jnp
from jax import lax
from jax.experimental import pallas as pl
from jax.experimental.pallas import tpu as pltpu
from jax.sharding import PartitionSpec as P

F32 = jnp.float32
BF = jnp.bfloat16
OMEGA = 2.0 / 3.0

SIDES = [(dx, dy) for dx in (-1, 0, 1) for dy in (-1, 0, 1) if dx or dy]


def there(dx, dy):
    gx, gy = lax.axis_index("gx"), lax.axis_index("gy")
    ok = jnp.bool_(True)
    if dx:
        ok &= (gx + dx >= 0) & (gx + dx < lax.axis_size("gx"))
    if dy:
        ok &= (gy + dy >= 0) & (gy + dy < lax.axis_size("gy"))
    return ok


def peer(dx, dy):
    return (lax.axis_index("gx") + dx, lax.axis_index("gy") + dy)


def remote(src, dst, send, recv, to):
    return pltpu.make_async_remote_copy(src_ref=src, dst_ref=dst, send_sem=send, recv_sem=recv, device_id=to, device_id_type=pl.DeviceIdType.MESH)


def greet():
    for dx, dy in SIDES:
        @pl.when(there(dx, dy))
        def _():
            pl.semaphore_signal(pltpu.get_barrier_semaphore(), inc=1, device_id=peer(dx, dy), device_id_type=pl.DeviceIdType.MESH)


def meet():
    gx, gy = lax.axis_index("gx"), lax.axis_index("gy")
    wide = 1 + (gx > 0).astype(jnp.int32) + (gx < lax.axis_size("gx") - 1).astype(jnp.int32)
    tall = 1 + (gy > 0).astype(jnp.int32) + (gy < lax.axis_size("gy") - 1).astype(jnp.int32)
    pl.semaphore_wait(pltpu.get_barrier_semaphore(), wide * tall - 1)


def exchange_start(copies):
    for s, (dx, dy) in enumerate(SIDES):
        @pl.when(there(dx, dy))
        def _():
            for c in copies(s, dx, dy, peer(dx, dy)):
                c.start()


def exchange_wait(copies):
    for s, (dx, dy) in enumerate(SIDES):
        @pl.when(there(-dx, -dy))
        def _():
            for c in copies(s, dx, dy, peer(dx, dy)):
                c.wait_recv()
    for s, (dx, dy) in enumerate(SIDES):
        @pl.when(there(dx, dy))
        def _():
            for c in copies(s, dx, dy, peer(dx, dy)):
                c.wait_send()


def exchange(copies):
    exchange_start(copies)
    exchange_wait(copies)


def halo_kernel(nx, ny, width, src, dst, send, recv):
    def taken(d, n):
        return {0: pl.ds(0, n), 1: pl.ds(n - width, width), -1: pl.ds(0, width)}[d]

    def landed(d, n):
        return {0: pl.ds(width, n), 1: pl.ds(0, width), -1: pl.ds(n + width, width)}[d]

    def copies(s, dx, dy, to):
        return [remote(src.at[taken(dx, nx), taken(dy, ny)], dst.at[landed(dx, nx), landed(dy, ny)], send.at[s], recv.at[s], to)]

    greet()
    meet()
    exchange(copies)


def halo_call(src, dst_shape, width):
    anyspec = pl.BlockSpec(memory_space=pl.ANY)
    return pl.pallas_call(functools.partial(halo_kernel, src.shape[0], src.shape[1], width),
        in_specs=[anyspec], out_specs=anyspec, out_shape=jax.ShapeDtypeStruct(dst_shape, src.dtype),
        scratch_shapes=[pltpu.SemaphoreType.DMA((8,)), pltpu.SemaphoreType.DMA((8,))],
        compiler_params=pltpu.CompilerParams(collective_id=1, has_side_effects=True), name="halo")(src)


def pick_blocks(pieces, block):
    out = pieces[3]
    for b in (2, 1, 0):
        out = jnp.where(block == b, pieces[b], out)
    return out


def turn(v, s):
    s = s % 4
    return v if s == 0 else pltpu.roll(v, 32*s, 1)


def gram_rows(x, p_buf, z_buf, g_buf, low_buf, slot):
    block16 = lax.broadcasted_iota(jnp.int32, (16,128), 1)//32
    block8 = lax.broadcasted_iota(jnp.int32, (8,128), 1)//32
    for half in range(2):
        p = [p_buf[x, 4*half+b] for b in range(4)]
        yh = jnp.concatenate([pick_blocks([turn(p[b], b-q) for b in range(4)], block16) for q in range(4)], axis=0)
        hi = yh.astype(BF)
        lo = (yh - hi.astype(F32)).astype(BF)
        o = lax.dot_general(jnp.concatenate([hi, lo, hi], axis=0), jnp.concatenate([hi, hi, lo], axis=0), (((0,),(0,)),((),())), preferred_element_type=F32)
        r = [pick_blocks([o[32*b+8*kb:32*b+8*kb+8] for b in range(4)], block8) * (1.0/64) for kb in range(4)]
        for b in range(4):
            z_buf[slot, :, b, :] = pick_blocks([turn(r[kb], kb-b) for kb in range(4)], block8)
        z = z_buf[slot]
        zh = z.astype(BF)
        g_buf[half, :, x] = zh
        low_buf[half, :, x] = (z - zh.astype(F32)).astype(BF)


def gram_kernel(nx, chunks, with_halo, *refs):
    if with_halo:
        b_ref, tile, gpad, glow, tiles, p_buf, z_buf, g_buf, low_buf, load, store, send, recv = refs
    else:
        b_ref, gpad, glow, p_buf, z_buf, g_buf, low_buf, load, store = refs
    part = nx // chunks
    loads = [[pltpu.make_async_copy(b_ref.at[pl.ds(c*part, part), :, y], p_buf.at[pl.ds(c*part, part), y], load.at[c, y]) for y in range(8)] for c in range(chunks)]
    for group in loads:
        for c in group: c.start()
    if with_halo:
        greet()
    for c in range(chunks):
        for one in loads[c]: one.wait()
        def rows(i, carry):
            for u in range(2):
                gram_rows(c*part + 2*i + u, p_buf, z_buf, g_buf, low_buf, u)
            return carry
        lax.fori_loop(0, part//2, rows, 0)
    mine = pltpu.make_async_copy(g_buf, gpad.at[pl.ds(1, 2), :, pl.ds(4, nx)], store.at[0])
    low = pltpu.make_async_copy(low_buf, glow, store.at[2])
    mine.start()
    low.start()
    if with_halo:
        meet()
        def strip(ref, sx, sy):
            return ref.at[sy, :, sx]
        def copies(s, dx, dy, to):
            sx = {0: pl.ds(0, nx), 1: pl.ds(nx-4, 4), -1: pl.ds(0, 4)}[dx]
            sy = {0: pl.ds(0, 2), 1: pl.ds(1, 1), -1: pl.ds(0, 1)}[dy]
            tx = {0: pl.ds(4, nx), 1: pl.ds(0, 4), -1: pl.ds(nx+4, 4)}[dx]
            ty = {0: pl.ds(1, 2), 1: pl.ds(0, 1), -1: pl.ds(3, 1)}[dy]
            return [remote(strip(g_buf, sx, sy), strip(gpad, tx, ty), send.at[0, s], recv.at[0, s], to),
                    remote(tile, tiles.at[1-dx, 1-dy], send.at[1, s], recv.at[1, s], to)]
        own_tile = pltpu.make_async_copy(tile, tiles.at[1, 1], store.at[1])
        own_tile.start()
        exchange(copies)
        own_tile.wait()
    mine.wait()
    low.wait()


def gram_call(nn, tile=None, chunks=4):
    nx = nn.shape[0]
    anyspec = pl.BlockSpec(memory_space=pl.ANY)
    gshape = jax.ShapeDtypeStruct((4, 8, nx+8, 4, 128), BF)
    scratch = [pltpu.VMEM((nx,8,16,128),F32), pltpu.VMEM((2,8,4,128),F32), pltpu.VMEM((2,8,nx,4,128),BF), pltpu.VMEM((2,8,nx,4,128),BF),
               pltpu.SemaphoreType.DMA((chunks,8)), pltpu.SemaphoreType.DMA((3,))]
    lshape = jax.ShapeDtypeStruct((2, 8, nx, 4, 128), BF)
    kern = functools.partial(gram_kernel, nx, chunks, tile is not None)
    if tile is None:
        return pl.pallas_call(kern, in_specs=[anyspec], out_specs=[anyspec]*2, out_shape=[gshape, lshape], scratch_shapes=scratch,
            compiler_params=pltpu.CompilerParams(vmem_limit_bytes=56<<20), name="gram")(nn)
    return pl.pallas_call(kern, in_specs=[anyspec]*2, out_specs=[anyspec]*3,
        out_shape=[gshape, lshape, jax.ShapeDtypeStruct((3,3)+tile.shape, tile.dtype)],
        scratch_shapes=scratch + [pltpu.SemaphoreType.DMA((2,8)), pltpu.SemaphoreType.DMA((2,8))],
        compiler_params=pltpu.CompilerParams(vmem_limit_bytes=56<<20, collective_id=0, has_side_effects=True), name="gram")(nn, tile)


def factor_kernel(nx, cells_ref, slot_ref, edge_ref, rid_ref, b_ref, g_ref, gl_ref, t_ref, tb_ref, comp, idcol, tab, bd, v_ref, g_buf, gl_buf, p_buf, t_buf, tb_buf, sem, load, store):
    ncell = cells_ref.shape[0]
    px = nx + 8
    els = rid_ref.shape[1]
    chunks = 4
    part = nx // chunks
    copies_g = [pltpu.make_async_copy(g_ref, g_buf, sem.at[0]), pltpu.make_async_copy(gl_ref, gl_buf, sem.at[1])]
    for c in copies_g: c.start()
    loads = [pltpu.make_async_copy(b_ref.at[:, :, y], p_buf.at[:, y], load.at[y]) for y in range(8)]
    for c in loads: c.start()
    def compact(i, n):
        cid = cells_ref[i]
        idcol[pl.ds(n, 1), :] = jnp.full((1, 128), cid, jnp.int32)
        comp[i] = n
        return n + (cid >= 0).astype(jnp.int32)
    n = lax.fori_loop(0, ncell, compact, 0, unroll=8)
    for c in copies_g: c.wait()
    @pl.when(edge_ref[0] == 1)
    def _(): g_buf[:, :, 0:4] = jnp.zeros((4, 8, 4, 4, 128), BF)
    @pl.when(edge_ref[1] == 1)
    def _(): g_buf[:, :, px-4:px] = jnp.zeros((4, 8, 4, 4, 128), BF)
    @pl.when(edge_ref[2] == 1)
    def _(): g_buf[0] = jnp.zeros((8, px, 4, 128), BF)
    @pl.when(edge_ref[3] == 1)
    def _(): g_buf[3] = jnp.zeros((8, px, 4, 128), BF)

    sub = lax.broadcasted_iota(jnp.int32, (32, 128), 0)
    block = lax.broadcasted_iota(jnp.int32, (32, 128), 1)//32
    def batch(bi, c):
        base = bi*128
        ids = idcol[pl.ds(base, 128), :]
        hot = [jnp.where(ids == rid_ref[:, 128*t:128*t+128], 1.0, 0.0).astype(BF) for t in range(els//128)]
        hot = jnp.concatenate(hot, axis=1)
        for k8 in range(8):
            g = jnp.concatenate([g_buf[yb, k8].reshape(px*4, 128) for yb in range(4)] + [gl_buf[yb, k8].reshape(nx*4, 128) for yb in range(2)], axis=0)
            s = jnp.dot(hot, g, preferred_element_type=F32).T
            for kb in range(4):
                v_ref[32*(8*kb+k8):32*(8*kb+k8)+32, :] = s[32*kb:32*kb+32]
        for jb in range(4):
            def pivot(j8, c2):
                j = jb*8 + j8
                row = v_ref[pl.ds(pl.multiple_of(j*32, 32), 32), :]
                d = lax.rsqrt(v_ref[pl.ds(j*33, 1), :])
                at_j = sub == j
                u = jnp.where(at_j, d, row*d)
                v_ref[pl.ds(pl.multiple_of(j*32, 32), 32), :] = u
                for i in range(jb*8, 32):
                    f = u[i:i+1, :]
                    old = v_ref[32*i:32*i+32, :]
                    if i < jb*8+8:
                        later = i > j
                        f = jnp.where(later, f, 0.0)
                        new = jnp.where(at_j & later, 0.0, old) - f*u
                        new = jnp.where(later, new, old)
                    else:
                        new = jnp.where(at_j, 0.0, old) - f*u
                    v_ref[32*i:32*i+32, :] = new
                return c2
            lax.fori_loop(0, 8, pivot, 0)
        for k in range(32):
            m = v_ref[pl.ds(k, 32, stride=32), :]
            m = jnp.where(sub >= k, m, 0.0)
            tab[k] = jnp.concatenate([m]*4, axis=0).T
        def spread(r, c2):
            w = tab[:, pl.ds(r, 1), :].reshape(32, 128)
            hi = w.astype(BF)
            lo = (w - hi.astype(F32)).astype(BF)
            for q in range(4):
                bd[base + r, 32*q:32*q+32, :] = jnp.where(block == q, hi, jnp.zeros_like(hi))
                bd[base + r, 128+32*q:160+32*q, :] = jnp.where(block == q, lo, jnp.zeros_like(lo))
            return c2
        lax.fori_loop(0, jnp.minimum(n - base, 128), spread, 0)
        return c
    lax.fori_loop(0, (n + 127)//128, batch, 0)

    for c in loads: c.wait()
    stores = []
    for ch in range(chunks):
        def one_x(i, c):
            x = ch*part + i
            for y in range(8):
                r = comp[slot_ref[x*8+y]]
                p = p_buf[x, y]
                ph = p.astype(BF)
                plo = (p - ph.astype(F32)).astype(BF)
                lhs = jnp.concatenate([jnp.concatenate([ph, ph], axis=1), jnp.concatenate([plo, jnp.zeros_like(plo)], axis=1)], axis=0)
                o = jnp.dot(lhs, bd[r], preferred_element_type=F32)
                t = o[:16] + o[16:]
                t_buf[x, y] = t
                tb_buf[x, y] = t.astype(BF)
            return c
        lax.fori_loop(0, part, one_x, 0)
        xs = pl.ds(ch*part, part)
        for c in (pltpu.make_async_copy(t_buf.at[xs], t_ref.at[xs], store.at[0, ch]), pltpu.make_async_copy(tb_buf.at[xs], tb_ref.at[xs], store.at[1, ch])):
            c.start()
            stores.append(c)
    for c in stores: c.wait()


def factor_call(cells, slots, edge, rid, nn, gpad, glow):
    nx = nn.shape[0]
    anyspec = pl.BlockSpec(memory_space=pl.ANY)
    nc = (nx+4)*12
    ncp = (nc + 127)//128*128
    return pl.pallas_call(functools.partial(factor_kernel, nx),
        grid_spec=pltpu.PrefetchScalarGridSpec(num_scalar_prefetch=3, grid=(1,),
          in_specs=[pl.BlockSpec(rid.shape, lambda i,*_: (0,0)), anyspec, anyspec, anyspec],
          out_specs=[anyspec, anyspec],
          scratch_shapes=[pltpu.SMEM((nc,), jnp.int32), pltpu.VMEM((ncp+128,128), jnp.int32), pltpu.VMEM((32,128,128),F32), pltpu.VMEM((ncp,256,128),BF),
             pltpu.VMEM((1024,128),F32), pltpu.VMEM(gpad.shape,BF), pltpu.VMEM(glow.shape,BF), pltpu.VMEM((nx,8,16,128),F32), pltpu.VMEM((nx,8,16,128),F32), pltpu.VMEM((nx,8,16,128),BF),
             pltpu.SemaphoreType.DMA((2,)), pltpu.SemaphoreType.DMA((8,)), pltpu.SemaphoreType.DMA((2,4))]),
        out_shape=[jax.ShapeDtypeStruct((nx,8,16,128),F32), jax.ShapeDtypeStruct((nx,8,16,128),BF)],
        compiler_params=pltpu.CompilerParams(vmem_limit_bytes=62<<20), name="factor")(cells, slots, edge, rid, nn, gpad, glow)


def apply_kernel(nx, px, py, xb, idx_ref, t_ref, d_ref, sel_ref, own_ref, tp_ref, a_ref, out_ref, abuf, table, wide, tall, scale_ref, tbuf, obuf, sems, osem, tsem):
    step = pl.program_id(0)
    steps = nx // xb
    slot = lax.rem(step, 2)
    def copies(s, slot):
        return [pltpu.make_async_copy(a_ref.at[pl.ds(s*xb, xb), :, :, ch, pl.ds(2*kp, 2), :], abuf.at[slot, :, :, kp, ch], sems.at[slot, 2*kp+ch]) for kp in range(2) for ch in range(2)]
    def outs(s, slot):
        return [pltpu.make_async_copy(obuf.at[slot, :, y], out_ref.at[pl.ds(s*xb, xb), :, y], osem.at[slot, y]) for y in range(8)]
    lane = lax.broadcasted_iota(jnp.int32, (16, 128), 1)
    @pl.when(step == 0)
    def _():
        strips = [(pl.ds(0, 2), pl.ds(0, py)), (pl.ds(px-2, 2), pl.ds(0, py)), (pl.ds(2, nx), pl.ds(0, 2)), (pl.ds(2, nx), pl.ds(py-2, 2))]
        fill = [pltpu.make_async_copy(tp_ref.at[sx, sy], tbuf.at[sx, sy], tsem.at[i]) for i, (sx, sy) in enumerate(strips)]
        fill.append(pltpu.make_async_copy(own_ref, tbuf.at[pl.ds(2, nx), pl.ds(2, py-4)], tsem.at[4]))
        for c in fill: c.start()
        for c in copies(0, 0): c.start()
        for c in fill: c.wait()
        def expand(x, carry):
            rows = tbuf[x].reshape(py*16, 128)
            o = jnp.dot(rows, sel_ref[...], preferred_element_type=F32)
            for y in range(py):
                for q in range(4):
                    tall[y, pl.ds(q, 16, stride=4), :] = o[y*16:(y+1)*16, q*128:(q+1)*128]
            for y in range(py):
                table[x*py+y] = tall[y].astype(BF)
            return carry
        lax.fori_loop(0, px, expand, 0)
    @pl.when(step + 1 < steps)
    def _():
        for c in copies(step+1, 1-slot): c.start()
    @pl.when(step >= 2)
    def _():
        for c in outs(step-2, slot): c.wait()
    for c in copies(step, slot): c.wait()
    row16 = lax.broadcasted_iota(jnp.int32, (16, 128), 0)
    col4 = (lax.broadcasted_iota(jnp.int32, (16, 128), 1) % 64) // 4
    pick = (lax.broadcasted_iota(jnp.int32, (64, 128), 0) % 4 == lax.broadcasted_iota(jnp.int32, (64, 128), 1) // 32)
    pick = jnp.where(pick, 1.0, 0.0).astype(BF)
    pick = jnp.concatenate([pick, pick], axis=0)
    lanew = lax.broadcasted_iota(jnp.int32, (64, 128), 1)
    def one_x(xi, carry):
        d = d_ref[xi] * OMEGA
        hi = d.astype(BF).astype(F32)
        both = jnp.concatenate([hi, d - hi], axis=1)
        spread = jnp.concatenate([jnp.where(row16 == col4, both[y:y+1], 0.0) for y in range(8)], axis=0)
        scale_ref[...] = jnp.dot(spread.astype(BF), pick, preferred_element_type=F32)
        for y in range(8):
            e4 = ((step*xb + xi)*8 + y)*4
            parts = []
            for kp in range(2):
                t0 = table[idx_ref[e4+2*kp]]
                t1 = table[idx_ref[e4+2*kp+1]]
                r = jnp.where(lanew < 64, t0, t1)
                parts.append(jnp.where((lanew//32) % 2 == 0, r, jnp.zeros_like(r)))
                parts.append(jnp.where((lanew//32) % 2 == 1, r, jnp.zeros_like(r)))
            rhs = jnp.concatenate(parts, axis=0)
            lhs = jnp.concatenate([abuf[slot, xi, y, 0].reshape(64,128), abuf[slot, xi, y, 1].reshape(64,128)], axis=1)
            wide[y] = jnp.dot(lhs, rhs, preferred_element_type=F32)
        for y in range(8):
            r = [[wide[y, pl.ds(32*ch+p, 16, stride=2), :] for p in range(2)] for ch in range(2)]
            u = jnp.where(lane < 64, r[0][0], r[1][1]) + pltpu.roll(jnp.where(lane < 64, r[1][0], r[0][1]), 64, 1)
            obuf[slot, xi, y] = t_ref[xi, y] - scale_ref[16*y:16*y+16, :] * u
        return carry
    lax.fori_loop(0, xb, one_x, 0)
    for c in outs(step, slot): c.start()
    @pl.when(step == steps - 1)
    def _():
        for c in outs(step-1, 1-slot) + outs(step, slot): c.wait()


def spread_matrix():
    r = jnp.arange(128)[:, None]; c = jnp.arange(512)[None, :]
    return ((r//32 == c//128) & (r%32 == c%32)).astype(BF)


def apply_call(idx, t4, d, own, tp, a6, xb=4):
    nx = t4.shape[0]; px, py = tp.shape[:2]
    anyspec = pl.BlockSpec(memory_space=pl.ANY)
    return pl.pallas_call(functools.partial(apply_kernel, nx, px, py, xb),
        grid_spec=pltpu.PrefetchScalarGridSpec(num_scalar_prefetch=1, grid=(nx//xb,),
          in_specs=[pl.BlockSpec((xb,8,16,128), lambda i,*_:(i,0,0,0)), pl.BlockSpec((xb,8,64), lambda i,*_:(i,0,0)), pl.BlockSpec((128,512), lambda i,*_:(0,0)),
                    anyspec, anyspec, anyspec],
          out_specs=anyspec,
          scratch_shapes=[pltpu.VMEM((2,xb,8,2,2,16,2,128),BF), pltpu.VMEM((px*py,64,128),BF), pltpu.VMEM((8,64,128),F32), pltpu.VMEM((py,64,128),F32), pltpu.VMEM((128,128),F32),
             pltpu.VMEM((px,py,16,128),BF), pltpu.VMEM((2,xb,8,16,128),F32), pltpu.SemaphoreType.DMA((2,4)), pltpu.SemaphoreType.DMA((2,8)), pltpu.SemaphoreType.DMA((5,))]),
        out_shape=jax.ShapeDtypeStruct((nx,16,8,128),F32),
        compiler_params=pltpu.CompilerParams(vmem_limit_bytes=56<<20), name="apply")(idx, t4, d, spread_matrix(), own, tp, a6)


def body(near_null, a_blocks, inv_diag, root_map, neighbours):
    nx, ny = root_map.shape
    grid_x, grid_y = nx * lax.axis_size("gx"), ny * lax.axis_size("gy")
    gx, gy = lax.axis_index("gx"), lax.axis_index("gy")
    sx, sy = gx * nx, gy * ny
    nn = near_null.reshape(nx, ny, 16, 128).transpose(0, 2, 1, 3)
    a6 = a_blocks.reshape(nx, ny, 4, 16, 2, 128).transpose(0, 1, 3, 4, 2, 5)
    tile = jnp.pad(root_map.T, ((0, 0), (0, 128 - nx)))
    gpad, glow, tiles = gram_call(nn, tile)
    around = tiles[:, :, :, :nx].transpose(0, 3, 1, 2).reshape(3 * nx, 3 * ny)[nx - 4:2 * nx + 4, ny - 4:2 * ny + 4]
    ax = sx - 4 + jnp.arange(nx + 8, dtype=jnp.int32)[:, None]
    ay = sy - 4 + jnp.arange(ny + 8, dtype=jnp.int32)[None, :]
    around = jnp.where((ax >= 0) & (ax < grid_x) & (ay >= 0) & (ay < grid_y), around, -1)
    cells = jnp.where(around == ax * grid_y + ay, around, -1)[2:-2, 2:-2].reshape(-1)
    rid = jnp.concatenate([around.reshape(nx + 8, 4, 4).transpose(1, 0, 2).reshape(1, -1), root_map.reshape(nx, 2, 4).transpose(1, 0, 2).reshape(1, -1)], axis=1)
    slots = ((root_map // grid_y - sx + 2) * (ny + 4) + root_map % grid_y - sy + 2).reshape(-1)
    edge = jnp.stack([gx == 0, gx == lax.axis_size("gx") - 1, gy == 0, gy == lax.axis_size("gy") - 1]).astype(jnp.int32)
    tent, low = factor_call(cells, slots, edge, rid, nn, gpad, glow)
    low_pad = halo_call(low, (nx + 4, ny + 4, 16, 128), 2)
    idx = ((neighbours // grid_y - sx + 2) * (ny + 4) + neighbours % grid_y - sy + 2).reshape(-1)
    out = apply_call(idx, tent, inv_diag, low, low_pad, a6)
    return out.transpose(0, 2, 1, 3).reshape(nx, ny, 2048)


def solution(mesh):
    in_specs = (P("gx", "gy", None), P("gx", "gy", None, None), P("gx", "gy", None), P("gx", "gy"), P("gx", "gy", None))
    return jax.shard_map(body, mesh=mesh, in_specs=in_specs, out_specs=P("gx", "gy", None), check_vma=False)
```

time: 171 us -> 103 us (0.60)
  Pallas kernels: 161 us -> 93.5 us
    pallas_call x3 -> x2, Pallas kernels: 97.3 us -> 34.1 us  [the longest x1 22.9 us: gram_call(): pl.pallas_call(kern, in_specs=[anyspec] * 2, out_specs=[anyspec] * 3, out...]
    pallas_call x1, Pallas kernels: 29.2 us -> 22.4 us  [factor_call(): pl.pallas_call(functools.partial(factor_kernel, nx), grid_spec=pltpu.Pref...]
    pallas_call x1, Pallas kernels: 34.3 us -> 37 us  [apply_call(): pl.pallas_call(functools.partial(apply_kernel, nx, px, py, xb), grid_spec...]
where the time goes in v1:
time: 103 us
  Pallas kernels  93.5 us (91%)
  local copies, waits for them, and re-layouts  5.86 us (6%)
  other arithmetic  3.6 us (3%)
    pallas_call x1, Pallas kernels, apply_call(): pl.pallas_call(functools.partial(apply_kernel, nx, px, py, xb), grid_spec...  37 us
    pallas_call x1, Pallas kernels, gram_call(): pl.pallas_call(kern, in_specs=[anyspec] * 2, out_specs=[anyspec] * 3, out...  22.9 us
    pallas_call x1, Pallas kernels, factor_call(): pl.pallas_call(functools.partial(factor_kernel, nx), grid_spec=pltpu.Pref...  22.4 us
    pallas_call x1, Pallas kernels, halo_call(): pl.pallas_call(functools.partial(halo_kernel, src.shape[0], src.shape[1],...  11.1 us

profile of v1, /device:TPU:7, one launch (start us, length us, event | category | flops | bytes accessed | tf_op | source)
XLA Modules:
  0.0 103.0 jit_solution(14389780921574003350)
XLA Ops:
  0.0 0.6 add_convert_fusion.edge_ref
  0.6 0.1 slice.13
  0.7 0.1 slice.14
  0.8 1.3 %pad.4.refs_1_ = s32[8,128]{1,0:T(8,128)} pad(s32[8,48]{1,0:T(8,128)} %bitcast.28, s32[]{:T(128)} %constant.111.clone.1), padding=0_0x0_80 | pad | bytes 5636 | tf_op jit(solution)/shard_map/jit(_pad)/pad | solution.py:397
  2.1 0.7 fusion.13
  2.8 0.8 fusion.5
  3.5 0.1 copy.10
  3.6 0.7 reshape.166.slot_ref
  4.3 0.8 copy.12
  5.1 0.1 reshape.170
  5.2 0.8 and_convert_fusion.sel_ref
  5.9 0.2 copy.7
  6.1 0.7 reshape.162.idx_ref
  6.8 22.9 %gram.1 = (bf16[4,8,56,4,128]{4,3,2,1,0:T(4,128)(2,1)}, bf16[2,8,48,4,128]{4,3,2,1,0:T(4,128)(2,1)}, s32[3,3,8,128]{3,2,1,0:T(8,128)}) custom-call(f32[48,16,8,128]{3,2,1,0:T(8,128)} %bitcast.23, s32[8,128]{1,0:T(8,128)} %pad.4.refs_1_), custom_call_target="tpu_custom_call" | custom-call | tf_op jit(solution)/shard_map/gram/pallas_call | solution.py:180
  29.8 0.8 slice_bitcast_fusion
  30.6 0.1 reshape.164
  30.6 0.1 slice_select_fusion
  30.7 0.1 compare_select_fusion
  30.8 0.1 copy.9
  30.9 0.7 reshape.165.cells_ref
  31.6 0.1 copy.11
  31.7 0.1 reshape.168
  31.8 0.6 pad_add_fusion.rid_ref
  32.4 22.4 %factor.1 = (f32[48,8,16,128]{3,2,1,0:T(8,128)}, bf16[48,8,16,128]{3,2,1,0:T(8,128)(2,1)}) custom-call(s32[624]{0:T(1024)} %reshape.165.cells_ref, s32[384]{0:T(512)} %reshape.166.slot_ref, s32[4]{0:T(128)} %add_convert_fusion.edge_ref, s32[1,1280]{1,0:T(1,128)} %pad_add_fusion.rid_ref, f32[48,16,8,128]{3,2,1,0:T(8,128)} %bitcast.24, ...), custom_call_target="tpu_custom_call" | custom-call | tf_op jit(solution)/shard_map/factor/pallas_call | solution.py:290
  54.8 11.1 %halo.1.tp_ref = bf16[52,12,16,128]{3,2,1,0:T(8,128)(2,1)} custom-call(bf16[48,8,16,128]{3,2,1,0:T(8,128)(2,1)} %get-tuple-element.14.src.own_ref), custom_call_target="tpu_custom_call" | custom-call | tf_op jit(solution)/shard_map/halo/pallas_call | solution.py:92
  66.0 37.0 %apply.1 = f32[48,16,8,128]{3,2,1,0:T(8,128)} custom-call(s32[1536]{0:T(1024)} %reshape.162.idx_ref, f32[48,8,16,128]{3,2,1,0:T(8,128)} %get-tuple-element.13.t_ref, f32[48,8,64]{2,1,0:T(8,128)} %d_ref.1, bf16[128,512]{1,0:T(8,128)(2,1)} %and_convert_fusion.sel_ref, bf16[48,8,16,128]{3,2,1,0:T(8,128)(2,1)} %get-tuple-element.14.src.own_ref, ...), custom_call_target="tpu_custom_call" | custom-call | tf_op jit(solution)/shard_map/apply/pallas_call | solution.py:379
  (7 shorter events, 0.0 us)

commit v2 on v1

v2 whole, which is shorter than its diff:
```python
import functools

import jax
import jax.numpy as jnp
from jax import lax
from jax.experimental import pallas as pl
from jax.experimental.pallas import tpu as pltpu
from jax.sharding import PartitionSpec as P

F32 = jnp.float32
BF = jnp.bfloat16
OMEGA = 2.0 / 3.0

SIDES = [(dx, dy) for dx in (-1, 0, 1) for dy in (-1, 0, 1) if dx or dy]


def there(dx, dy):
    gx, gy = lax.axis_index("gx"), lax.axis_index("gy")
    ok = jnp.bool_(True)
    if dx:
        ok &= (gx + dx >= 0) & (gx + dx < lax.axis_size("gx"))
    if dy:
        ok &= (gy + dy >= 0) & (gy + dy < lax.axis_size("gy"))
    return ok


def peer(dx, dy):
    return (lax.axis_index("gx") + dx, lax.axis_index("gy") + dy)


def remote(src, dst, send, recv, to):
    return pltpu.make_async_remote_copy(src_ref=src, dst_ref=dst, send_sem=send, recv_sem=recv, device_id=to, device_id_type=pl.DeviceIdType.MESH)


def greet():
    for dx, dy in SIDES:
        @pl.when(there(dx, dy))
        def _():
            pl.semaphore_signal(pltpu.get_barrier_semaphore(), inc=1, device_id=peer(dx, dy), device_id_type=pl.DeviceIdType.MESH)


def meet():
    gx, gy = lax.axis_index("gx"), lax.axis_index("gy")
    wide = 1 + (gx > 0).astype(jnp.int32) + (gx < lax.axis_size("gx") - 1).astype(jnp.int32)
    tall = 1 + (gy > 0).astype(jnp.int32) + (gy < lax.axis_size("gy") - 1).astype(jnp.int32)
    pl.semaphore_wait(pltpu.get_barrier_semaphore(), wide * tall - 1)


def send_all(messages, phase):
    for at, dx, dy, copy in messages:
        if at == phase:
            @pl.when(there(dx, dy))
            def _():
                copy(peer(dx, dy)).start()


def wait_all(messages):
    for _, dx, dy, copy in messages:
        @pl.when(there(-dx, -dy))
        def _():
            copy(peer(dx, dy)).wait_recv()
    for _, dx, dy, copy in messages:
        @pl.when(there(dx, dy))
        def _():
            copy(peer(dx, dy)).wait_send()


def spread_lanes():
    r = lax.broadcasted_iota(jnp.int32, (128, 512), 0)
    c = lax.broadcasted_iota(jnp.int32, (128, 512), 1)
    return jnp.where((r // 32 == c // 128) & (r % 32 == c % 32), 1.0, 0.0).astype(BF)


def expanded(rows, fan_ref, tall):
    o = jnp.dot(rows, fan_ref[...], preferred_element_type=F32)
    for e in range(rows.shape[0] // 16):
        for q in range(4):
            tall[e, pl.ds(q, 16, stride=4), :] = o[e*16:(e+1)*16, q*128:(q+1)*128]
    return [tall[e].astype(BF) for e in range(rows.shape[0] // 16)]


def halo_kernel(nx, ny, width, src, dst, own_table, buf, table, fan_ref, tall, load, store, send, recv):
    def taken(d, n):
        return {0: pl.ds(0, n), 1: pl.ds(n - width, width), -1: pl.ds(0, width)}[d]

    def landed(d, n):
        return {0: pl.ds(width, n), 1: pl.ds(0, width), -1: pl.ds(n + width, width)}[d]

    def message(s, dx, dy):
        return (0, dx, dy, lambda to: remote(src.at[taken(dx, nx), taken(dy, ny)], dst.at[landed(dx, nx), landed(dy, ny)], send.at[s], recv.at[s], to))

    messages = [message(s, dx, dy) for s, (dx, dy) in enumerate(SIDES)]
    greet()
    fill = pltpu.make_async_copy(src, buf, load.at[0])
    fill.start()
    fan_ref[...] = spread_lanes()
    meet()
    send_all(messages, 0)
    fill.wait()
    chunks = 4
    part = nx // chunks
    stores = []
    for c in range(chunks):
        def expand(i, carry):
            x = c*part + i
            for y, t in enumerate(expanded(buf[x].reshape(ny*16, 128), fan_ref, tall)):
                table[x, y] = t
            return carry
        lax.fori_loop(0, part, expand, 0)
        xs = pl.ds(c*part, part)
        stores.append(pltpu.make_async_copy(table.at[xs], own_table.at[xs], store.at[c]))
        stores[-1].start()
    wait_all(messages)
    for s in stores:
        s.wait()


def halo_call(src, dst_shape, width):
    anyspec = pl.BlockSpec(memory_space=pl.ANY)
    nx, ny = src.shape[:2]
    return pl.pallas_call(functools.partial(halo_kernel, nx, ny, width),
        in_specs=[anyspec], out_specs=[anyspec]*2, out_shape=[jax.ShapeDtypeStruct(dst_shape, src.dtype), jax.ShapeDtypeStruct((nx, ny, 64, 128), BF)],
        scratch_shapes=[pltpu.VMEM(src.shape, BF), pltpu.VMEM((nx, ny, 64, 128), BF), pltpu.VMEM((128, 512), BF), pltpu.VMEM((ny, 64, 128), F32),
                        pltpu.SemaphoreType.DMA((1,)), pltpu.SemaphoreType.DMA((4,)), pltpu.SemaphoreType.DMA((8,)), pltpu.SemaphoreType.DMA((8,))],
        compiler_params=pltpu.CompilerParams(vmem_limit_bytes=40<<20, collective_id=1, has_side_effects=True), name="halo")(src)


def pick_blocks(pieces, block):
    out = pieces[3]
    for b in (2, 1, 0):
        out = jnp.where(block == b, pieces[b], out)
    return out


def turn(v, s):
    s = s % 4
    return v if s == 0 else pltpu.roll(v, 32*s, 1)


def gram_rows(x, p_buf, z_buf, g_buf, low_buf, slot):
    block16 = lax.broadcasted_iota(jnp.int32, (16,128), 1)//32
    block8 = lax.broadcasted_iota(jnp.int32, (8,128), 1)//32
    for half in range(2):
        p = [p_buf[x, 4*half+b] for b in range(4)]
        yh = jnp.concatenate([pick_blocks([turn(p[b], b-q) for b in range(4)], block16) for q in range(4)], axis=0)
        hi = yh.astype(BF)
        lo = (yh - hi.astype(F32)).astype(BF)
        o = lax.dot_general(jnp.concatenate([hi, lo, hi], axis=0), jnp.concatenate([hi, hi, lo], axis=0), (((0,),(0,)),((),())), preferred_element_type=F32)
        r = [pick_blocks([o[32*b+8*kb:32*b+8*kb+8] for b in range(4)], block8) * (1.0/64) for kb in range(4)]
        for b in range(4):
            z_buf[slot, :, b, :] = pick_blocks([turn(r[kb], kb-b) for kb in range(4)], block8)
        z = z_buf[slot]
        zh = z.astype(BF)
        g_buf[half, :, x] = zh
        low_buf[half, :, x] = (z - zh.astype(F32)).astype(BF)


def gram_kernel(nx, chunks, with_halo, *refs):
    if with_halo:
        b_ref, tile, gpad, glow, tiles, p_buf, z_buf, g_buf, low_buf, load, store, send, recv = refs
    else:
        b_ref, gpad, glow, p_buf, z_buf, g_buf, low_buf, load, store = refs
    part = nx // chunks
    loads = [[pltpu.make_async_copy(b_ref.at[pl.ds(c*part, part), :, y], p_buf.at[pl.ds(c*part, part), y], load.at[c, y]) for y in range(8)] for c in range(chunks)]
    for group in loads:
        for c in group: c.start()
    messages = []
    if with_halo:
        def block(phase, dx, dy, sx, tx):
            sy = {0: pl.ds(0, 2), 1: pl.ds(1, 1), -1: pl.ds(0, 1)}[dy]
            ty = {0: pl.ds(1, 2), 1: pl.ds(0, 1), -1: pl.ds(3, 1)}[dy]
            s = len(messages)
            messages.append((phase, dx, dy, lambda to: remote(g_buf.at[sy, :, sx], gpad.at[ty, :, tx], send.at[s], recv.at[s], to)))
        def roots(dx, dy):
            s = len(messages)
            messages.append((0, dx, dy, lambda to: remote(tile, tiles.at[1-dx, 1-dy], send.at[s], recv.at[s], to)))
        for dx, dy in SIDES:
            roots(dx, dy)
        for dy in (-1, 0, 1):
            block(0, -1, dy, pl.ds(0, 4), pl.ds(nx+4, 4))
            block(chunks-1, 1, dy, pl.ds(nx-4, 4), pl.ds(0, 4))
        for c in range(chunks):
            for dy in (-1, 1):
                block(c, 0, dy, pl.ds(c*part, part), pl.ds(4 + c*part, part))
        greet()
    for c in range(chunks):
        for one in loads[c]: one.wait()
        def rows(i, carry):
            for u in range(2):
                gram_rows(c*part + 2*i + u, p_buf, z_buf, g_buf, low_buf, u)
            return carry
        lax.fori_loop(0, part//2, rows, 0)
        if with_halo:
            if c == 0:
                meet()
            send_all(messages, c)
    mine = [pltpu.make_async_copy(g_buf, gpad.at[pl.ds(1, 2), :, pl.ds(4, nx)], store.at[0]), pltpu.make_async_copy(low_buf, glow, store.at[1])]
    if with_halo:
        mine.append(pltpu.make_async_copy(tile, tiles.at[1, 1], store.at[2]))
    for c in mine: c.start()
    if with_halo:
        wait_all(messages)
    for c in mine: c.wait()


def gram_call(nn, tile=None, chunks=4):
    nx = nn.shape[0]
    anyspec = pl.BlockSpec(memory_space=pl.ANY)
    gshape = jax.ShapeDtypeStruct((4, 8, nx+8, 4, 128), BF)
    scratch = [pltpu.VMEM((nx,8,16,128),F32), pltpu.VMEM((2,8,4,128),F32), pltpu.VMEM((2,8,nx,4,128),BF), pltpu.VMEM((2,8,nx,4,128),BF),
               pltpu.SemaphoreType.DMA((chunks,8)), pltpu.SemaphoreType.DMA((3,))]
    lshape = jax.ShapeDtypeStruct((2, 8, nx, 4, 128), BF)
    kern = functools.partial(gram_kernel, nx, chunks, tile is not None)
    if tile is None:
        return pl.pallas_call(kern, in_specs=[anyspec], out_specs=[anyspec]*2, out_shape=[gshape, lshape], scratch_shapes=scratch,
            compiler_params=pltpu.CompilerParams(vmem_limit_bytes=56<<20), name="gram")(nn)
    return pl.pallas_call(kern, in_specs=[anyspec]*2, out_specs=[anyspec]*3,
        out_shape=[gshape, lshape, jax.ShapeDtypeStruct((3,3)+tile.shape, tile.dtype)],
        scratch_shapes=scratch + [pltpu.SemaphoreType.DMA((14 + 2*chunks,)), pltpu.SemaphoreType.DMA((14 + 2*chunks,))],
        compiler_params=pltpu.CompilerParams(vmem_limit_bytes=56<<20, collective_id=0, has_side_effects=True), name="gram")(nn, tile)


def local_slots(nx, ny):
    grid_y = ny * lax.axis_size("gy")
    first_x, first_y = lax.axis_index("gx")*nx - 2, lax.axis_index("gy")*ny - 2
    bits = grid_y.bit_length() - 1

    def place(flat):
        x = lax.shift_right_logical(flat, bits) if grid_y == 1 << bits else lax.div(flat, grid_y)
        return x - first_x, flat - x*grid_y - first_y
    return place


def factor_kernel(nx, cells_ref, root_ref, rid_ref, b_ref, g_ref, gl_ref, t_ref, tb_ref, comp, idcol, tab, bd, v_ref, g_buf, gl_buf, p_buf, t_buf, tb_buf, sem, load, store):
    ncell = cells_ref.shape[0]
    px = nx + 8
    gx, gy = lax.axis_index("gx"), lax.axis_index("gy")
    place = local_slots(nx, 8)
    els = rid_ref.shape[1]
    chunks = 4
    part = nx // chunks
    copies_g = [pltpu.make_async_copy(g_ref, g_buf, sem.at[0]), pltpu.make_async_copy(gl_ref, gl_buf, sem.at[1])]
    for c in copies_g: c.start()
    loads = [pltpu.make_async_copy(b_ref.at[:, :, y], p_buf.at[:, y], load.at[y]) for y in range(8)]
    for c in loads: c.start()
    def compact(i, n):
        cid = cells_ref[i]
        idcol[pl.ds(n, 1), :] = jnp.full((1, 128), cid, jnp.int32)
        comp[i] = n
        return n + (cid >= 0).astype(jnp.int32)
    n = lax.fori_loop(0, ncell, compact, 0, unroll=8)
    for c in copies_g: c.wait()
    @pl.when(gx == 0)
    def _(): g_buf[:, :, 0:16] = jnp.zeros((4, 8, 16, 128), BF)
    @pl.when(gx == lax.axis_size("gx") - 1)
    def _(): g_buf[:, :, 4*px-16:4*px] = jnp.zeros((4, 8, 16, 128), BF)
    @pl.when(gy == 0)
    def _(): g_buf[0] = jnp.zeros((8, 4*px, 128), BF)
    @pl.when(gy == lax.axis_size("gy") - 1)
    def _(): g_buf[3] = jnp.zeros((8, 4*px, 128), BF)

    sub = lax.broadcasted_iota(jnp.int32, (32, 128), 0)
    block = lax.broadcasted_iota(jnp.int32, (32, 128), 1)//32
    def batch(bi, c):
        base = bi*128
        ids = idcol[pl.ds(base, 128), :]
        hot = [jnp.where(ids == rid_ref[:, 128*t:128*t+128], 1.0, 0.0).astype(BF) for t in range(els//128)]
        hot = jnp.concatenate(hot, axis=1)
        for k8 in range(8):
            g = jnp.concatenate([g_buf[yb, k8] for yb in range(4)] + [gl_buf[yb, k8] for yb in range(2)], axis=0)
            s = jnp.dot(hot, g, preferred_element_type=F32).T
            for kb in range(4):
                v_ref[32*(8*kb+k8):32*(8*kb+k8)+32, :] = s[32*kb:32*kb+32]
        for jb in range(4):
            def pivot(j8, c2):
                j = jb*8 + j8
                row = v_ref[pl.ds(pl.multiple_of(j*32, 32), 32), :]
                d = lax.rsqrt(v_ref[pl.ds(j*33, 1), :])
                at_j = sub == j
                u = jnp.where(at_j, d, row*d)
                v_ref[pl.ds(pl.multiple_of(j*32, 32), 32), :] = u
                for i in range(jb*8, 32):
                    f = u[i:i+1, :]
                    old = v_ref[32*i:32*i+32, :]
                    if i < jb*8+8:
                        later = i > j
                        f = jnp.where(later, f, 0.0)
                        new = jnp.where(at_j & later, 0.0, old) - f*u
                        new = jnp.where(later, new, old)
                    else:
                        new = jnp.where(at_j, 0.0, old) - f*u
                    v_ref[32*i:32*i+32, :] = new
                return c2
            lax.fori_loop(0, 8, pivot, 0)
        for k in range(32):
            m = v_ref[pl.ds(k, 32, stride=32), :]
            m = jnp.where(sub >= k, m, 0.0)
            tab[k] = jnp.concatenate([m]*4, axis=0).T
        def spread(i, c2):
            for u in range(4):
                r = 4*i + u
                w = tab[:, pl.ds(r, 1), :].reshape(32, 128)
                hi = w.astype(BF).astype(F32)
                lo = w - hi
                bd[base + r, 0:128, :] = jnp.concatenate([jnp.where(block == q, hi, 0.0) for q in range(4)], axis=0).astype(BF)
                bd[base + r, 128:256, :] = jnp.concatenate([jnp.where(block == q, lo, 0.0) for q in range(4)], axis=0).astype(BF)
            return c2
        lax.fori_loop(0, (jnp.minimum(n - base, 128) + 3)//4, spread, 0)
        return c
    lax.fori_loop(0, (n + 127)//128, batch, 0)

    for c in loads: c.wait()
    stores = []
    for ch in range(chunks):
        def one_x(i, c):
            x = ch*part + i
            for y in range(8):
                rx, ry = place(root_ref[y, x])
                r = comp[rx*12 + ry]
                p = p_buf[x, y]
                ph = p.astype(BF)
                plo = (p - ph.astype(F32)).astype(BF)
                lhs = jnp.concatenate([jnp.concatenate([ph, ph], axis=1), jnp.concatenate([plo, jnp.zeros_like(plo)], axis=1)], axis=0)
                o = jnp.dot(lhs, bd[r], preferred_element_type=F32)
                t = o[:16] + o[16:]
                t_buf[x, y] = t
                tb_buf[x, y] = t.astype(BF)
            return c
        lax.fori_loop(0, part, one_x, 0)
        xs = pl.ds(ch*part, part)
        for c in (pltpu.make_async_copy(t_buf.at[xs], t_ref.at[xs], store.at[0, ch]), pltpu.make_async_copy(tb_buf.at[xs], tb_ref.at[xs], store.at[1, ch])):
            c.start()
            stores.append(c)
    for c in stores: c.wait()


def factor_call(cells, roots, rid, nn, gpad, glow):
    nx = nn.shape[0]
    anyspec = pl.BlockSpec(memory_space=pl.ANY)
    nc = (nx+4)*12
    ncp = (nc + 127)//128*128
    return pl.pallas_call(functools.partial(factor_kernel, nx),
        grid_spec=pltpu.PrefetchScalarGridSpec(num_scalar_prefetch=2, grid=(1,),
          in_specs=[pl.BlockSpec(rid.shape, lambda i,*_: (0,0)), anyspec, anyspec, anyspec],
          out_specs=[anyspec, anyspec],
          scratch_shapes=[pltpu.SMEM((nc,), jnp.int32), pltpu.VMEM((ncp+128,128), jnp.int32), pltpu.VMEM((32,128,128),F32), pltpu.VMEM((ncp,256,128),BF),
             pltpu.VMEM((1024,128),F32), pltpu.VMEM(gpad.shape,BF), pltpu.VMEM(glow.shape,BF), pltpu.VMEM((nx,8,16,128),F32), pltpu.VMEM((nx,8,16,128),F32), pltpu.VMEM((nx,8,16,128),BF),
             pltpu.SemaphoreType.DMA((2,)), pltpu.SemaphoreType.DMA((8,)), pltpu.SemaphoreType.DMA((2,4))]),
        out_shape=[jax.ShapeDtypeStruct((nx,8,16,128),F32), jax.ShapeDtypeStruct((nx,8,16,128),BF)],
        compiler_params=pltpu.CompilerParams(vmem_limit_bytes=62<<20), name="factor")(cells, roots, rid, nn, gpad, glow)


def apply_kernel(nx, px, py, xb, idx_ref, t_ref, d_ref, own_ref, tp_ref, a_ref, out_ref, abuf, table, wide, tall, fan_ref, scale_ref, tbuf, obuf, sems, osem, tsem):
    step = pl.program_id(0)
    steps = nx // xb
    slot = lax.rem(step, 2)
    def fetch(s, slot):
        for c in range(32):
            for kp in range(2):
                pltpu.make_async_copy(a_ref.at[pl.ds(s*xb, xb), :, c, pl.ds(2*kp, 2), :], abuf.at[slot, :, :, kp, pl.ds(32*(c % 2) + 2*(c//2), 2), :], sems.at[slot]).start()
    def outs(s, slot):
        return [pltpu.make_async_copy(obuf.at[slot, :, y], out_ref.at[pl.ds(s*xb, xb), :, y], osem.at[slot, y]) for y in range(8)]
    lane = lax.broadcasted_iota(jnp.int32, (16, 128), 1)
    place = local_slots(nx, 8)
    def load_at(flat):
        tx, ty = place(flat)
        return table[tx, ty]
    @pl.when(step == 0)
    def _():
        strips = [(pl.ds(0, 2), pl.ds(0, py)), (pl.ds(px-2, 2), pl.ds(0, py)), (pl.ds(2, nx), pl.ds(0, 2)), (pl.ds(2, nx), pl.ds(py-2, 2))]
        fill = [pltpu.make_async_copy(tp_ref.at[sx, sy], tbuf.at[sx, sy], tsem.at[i]) for i, (sx, sy) in enumerate(strips)]
        own = pltpu.make_async_copy(own_ref, table.at[pl.ds(2, nx), pl.ds(2, py-4)], tsem.at[4])
        for c in fill: c.start()
        own.start()
        fetch(0, 0)
        fan_ref[...] = spread_lanes()
        for c in fill: c.wait()
        def ends(i, carry):
            x = jnp.where(i < 2, i, px - 4 + i)
            for y, t in enumerate(expanded(tbuf[x].reshape(py*16, 128), fan_ref, tall)):
                table[x, y] = t
            return carry
        lax.fori_loop(0, 4, ends, 0)
        def sides(i, carry):
            at = [(2 + 3*i + u, y) for u in range(3) for y in (0, 1, py-2, py-1)]
            rows = jnp.concatenate([tbuf[x, y] for x, y in at], axis=0)
            for (x, y), t in zip(at, expanded(rows, fan_ref, tall)):
                table[x, y] = t
            return carry
        lax.fori_loop(0, nx//3, sides, 0)
        own.wait()
    @pl.when(step + 1 < steps)
    def _():
        fetch(step+1, 1-slot)
    @pl.when(step >= 2)
    def _():
        for c in outs(step-2, slot): c.wait()
    pltpu.make_async_copy(abuf.at[slot], abuf.at[slot], sems.at[slot]).wait()
    row16 = lax.broadcasted_iota(jnp.int32, (16, 128), 0)
    col4 = (lax.broadcasted_iota(jnp.int32, (16, 128), 1) % 64) // 4
    pick = (lax.broadcasted_iota(jnp.int32, (64, 128), 0) % 4 == lax.broadcasted_iota(jnp.int32, (64, 128), 1) // 32)
    pick = jnp.where(pick, 1.0, 0.0).astype(BF)
    pick = jnp.concatenate([pick, pick], axis=0)
    lanew = lax.broadcasted_iota(jnp.int32, (64, 128), 1)
    def one_x(xi, carry):
        d = d_ref[xi] * OMEGA
        hi = d.astype(BF).astype(F32)
        both = jnp.concatenate([hi, d - hi], axis=1)
        spread = jnp.concatenate([jnp.where(row16 == col4, both[y:y+1], 0.0) for y in range(8)], axis=0)
        scale_ref[...] = jnp.dot(spread.astype(BF), pick, preferred_element_type=F32)
        for y in range(8):
            x = step*xb + xi
            parts = []
            for kp in range(2):
                t0 = load_at(idx_ref[y, 2*kp, x])
                t1 = load_at(idx_ref[y, 2*kp+1, x])
                r = jnp.where(lanew < 64, t0, t1)
                parts.append(jnp.where((lanew//32) % 2 == 0, r, jnp.zeros_like(r)))
                parts.append(jnp.where((lanew//32) % 2 == 1, r, jnp.zeros_like(r)))
            rhs = jnp.concatenate(parts, axis=0)
            lhs = jnp.concatenate([abuf[slot, xi, y, 0], abuf[slot, xi, y, 1]], axis=1)
            wide[y] = jnp.dot(lhs, rhs, preferred_element_type=F32)
        for y in range(8):
            r = [[wide[y, pl.ds(32*ch+p, 16, stride=2), :] for p in range(2)] for ch in range(2)]
            u = jnp.where(lane < 64, r[0][0], r[1][1]) + pltpu.roll(jnp.where(lane < 64, r[1][0], r[0][1]), 64, 1)
            obuf[slot, xi, y] = t_ref[xi, y] - scale_ref[16*y:16*y+16, :] * u
        return carry
    lax.fori_loop(0, xb, one_x, 0)
    for c in outs(step, slot): c.start()
    @pl.when(step == steps - 1)
    def _():
        for c in outs(step-1, 1-slot) + outs(step, slot): c.wait()


def apply_call(idx, t4, d, own, tp, a6, xb=12):
    nx = t4.shape[0]; px, py = tp.shape[:2]
    anyspec = pl.BlockSpec(memory_space=pl.ANY)
    return pl.pallas_call(functools.partial(apply_kernel, nx, px, py, xb),
        grid_spec=pltpu.PrefetchScalarGridSpec(num_scalar_prefetch=1, grid=(nx//xb,),
          in_specs=[pl.BlockSpec((xb,8,16,128), lambda i,*_:(i,0,0,0)), pl.BlockSpec((xb,8,64), lambda i,*_:(i,0,0)),
                    anyspec, anyspec, anyspec],
          out_specs=anyspec,
          scratch_shapes=[pltpu.VMEM((2,xb,8,2,64,128),BF), pltpu.VMEM((px,py,64,128),BF), pltpu.VMEM((8,64,128),F32), pltpu.VMEM((12,64,128),F32), pltpu.VMEM((128,512),BF), pltpu.VMEM((128,128),F32),
             pltpu.VMEM((px,py,16,128),BF), pltpu.VMEM((2,xb,8,16,128),F32), pltpu.SemaphoreType.DMA((2,)), pltpu.SemaphoreType.DMA((2,8)), pltpu.SemaphoreType.DMA((5,))]),
        out_shape=jax.ShapeDtypeStruct((nx,16,8,128),F32),
        compiler_params=pltpu.CompilerParams(vmem_limit_bytes=56<<20), name="apply")(idx, t4, d, own, tp, a6)


def body(near_null, a_blocks, inv_diag, root_map, neighbours):
    nx, ny = root_map.shape
    grid_x, grid_y = nx * lax.axis_size("gx"), ny * lax.axis_size("gy")
    gx, gy = lax.axis_index("gx"), lax.axis_index("gy")
    sx, sy = gx * nx, gy * ny
    nn = near_null.reshape(nx, ny, 16, 128).transpose(0, 2, 1, 3)
    a5 = a_blocks.reshape(nx, ny, 4, 32, 128).transpose(0, 1, 3, 2, 4)
    roots = root_map.T
    gpad, glow, tiles = gram_call(nn, roots)
    around = tiles.transpose(0, 3, 1, 2).reshape(3 * nx, 3 * ny)[nx - 4:2 * nx + 4, ny - 4:2 * ny + 4]
    ax = sx - 4 + jnp.arange(nx + 8, dtype=jnp.int32)[:, None]
    ay = sy - 4 + jnp.arange(ny + 8, dtype=jnp.int32)[None, :]
    around = jnp.where((ax >= 0) & (ax < grid_x) & (ay >= 0) & (ay < grid_y), around, -1)
    cells = jnp.where(around == ax * grid_y + ay, around, -1)[2:-2, 2:-2].reshape(-1)
    rid = jnp.concatenate([around.reshape(nx + 8, 4, 4).transpose(1, 0, 2).reshape(1, -1), root_map.reshape(nx, 2, 4).transpose(1, 0, 2).reshape(1, -1)], axis=1)
    tent, low = factor_call(cells, roots, rid, nn, gpad.reshape(4, 8, -1, 128), glow.reshape(2, 8, -1, 128))
    low_pad, own_table = halo_call(low, (nx + 4, ny + 4, 16, 128), 2)
    out = apply_call(neighbours.transpose(1, 2, 0), tent, inv_diag, own_table, low_pad, a5)
    return out.transpose(0, 2, 1, 3).reshape(nx, ny, 2048)


def solution(mesh):
    in_specs = (P("gx", "gy", None), P("gx", "gy", None, None), P("gx", "gy", None), P("gx", "gy"), P("gx", "gy", None))
    return jax.shard_map(body, mesh=mesh, in_specs=in_specs, out_specs=P("gx", "gy", None), check_vma=False)
```

time: 103 us -> 93.4 us (0.907)
  Pallas kernels: 93.5 us -> 83.5 us
  other arithmetic: 3.6 us -> 0.78 us
  local copies, waits for them, and re-layouts: 5.86 us -> 8.43 us
    pallas_call x1, Pallas kernels: 37 us -> 29.9 us  [apply_call(): pl.pallas_call(functools.partial(apply_kernel, nx, px, py, xb), grid_spec...]
    unnamed x0 -> x6, local copies, waits for them, and re-layouts: none -> 5.51 us
    pallas_call x1, Pallas kernels: 22.4 us -> 20.3 us  [factor_call(): pl.pallas_call(functools.partial(factor_kernel, nx), grid_spec=pltpu.Pref...]
    add x2 -> x0, other arithmetic: 1.47 us -> none  [the longest x1 0.76 us: body(): (neighbours // grid_y - sx + 2) * (ny + 4) + neighbours % grid_y - sy + 2]
    reshape x3 -> x1, local copies, waits for them, and re-layouts: 1.49 us -> 0.08 us  [body(): tiles.transpose(0, 3, 1, 2).reshape(3 * nx, 3 * ny)]
    convert_element_type x2 -> x0, other arithmetic: 1.35 us -> none  [the longest x1 0.76 us: spread_matrix(): return ((r // 32 == c // 128) & (r % 32 == c % 32)).astype(BF)]
    pallas_call x1, Pallas kernels: 22.9 us -> 21.6 us  [gram_call(): pl.pallas_call(kern, in_specs=[anyspec] * 2, out_specs=[anyspec] * 3, out...]
    pad x1 -> x0, local copies, waits for them, and re-layouts: 1.28 us -> none  [body(): tile = jnp.pad(root_map.T, ((0, 0), (0, 128 - nx)))]
where the time goes in v2:
time: 93.4 us; the launch traced here: 92.8 us
  Pallas kernels  83.5 us (89%)
  local copies, waits for them, and re-layouts  8.43 us (9%)
    pallas_call x1, Pallas kernels, apply_call(): pl.pallas_call(functools.partial(apply_kernel, nx, px, py, xb), grid_spec...  29.9 us
    pallas_call x1, Pallas kernels, gram_call(): pl.pallas_call(kern, in_specs=[anyspec] * 2, out_specs=[anyspec] * 3, out...  21.6 us
    pallas_call x1, Pallas kernels, factor_call(): pl.pallas_call(functools.partial(factor_kernel, nx), grid_spec=pltpu.Pref...  20.3 us
    pallas_call x1, Pallas kernels, halo_call(): pl.pallas_call(functools.partial(halo_kernel, nx, ny, width), in_specs=[a...  11.7 us
    unnamed x6, local copies, waits for them, and re-layouts  5.51 us

profile of v2, /device:TPU:7, one launch (start us, length us, event | category | flops | bytes accessed | tf_op | source)
XLA Modules:
  0.0 92.8 jit_solution(7155091720464772541)
XLA Ops:
  0.0 0.1 slice.9
  0.1 0.1 slice.10
  0.2 0.8 copy.10
  1.0 0.1 reshape.64
  1.1 21.6 %gram.1 = (bf16[4,8,56,4,128]{4,3,2,1,0:T(4,128)(2,1)}, bf16[2,8,48,4,128]{4,3,2,1,0:T(4,128)(2,1)}, s32[3,3,8,48]{3,2,1,0:T(8,128)}) custom-call(f32[48,16,8,128]{3,2,1,0:T(8,128)} %bitcast.22, s32[8,48]{1,0:T(8,128)} %bitcast.30), custom_call_target="tpu_custom_call" | custom-call | tf_op jit(solution)/shard_map/gram/pallas_call | solution.py:217
  22.7 0.8 copy.7
  23.4 0.1 reshape.59
  23.5 0.1 slice_select_fusion
  23.6 0.1 compare_select_fusion
  23.7 0.1 copy.8
  23.8 0.7 reshape.60.cells_ref
  24.5 0.1 copy.9
  24.6 0.1 reshape.62
  24.7 0.6 pad_add_fusion.rid_ref
  25.3 20.3 %factor.1 = (f32[48,8,16,128]{3,2,1,0:T(8,128)}, bf16[48,8,16,128]{3,2,1,0:T(8,128)(2,1)}) custom-call(s32[624]{0:T(1024)} %reshape.60.cells_ref, s32[8,48]{1,0:T(8,128)} %bitcast.31, s32[1,1280]{1,0:T(1,128)} %pad_add_fusion.rid_ref, f32[48,16,8,128]{3,2,1,0:T(8,128)} %bitcast.23, bf16[4,8,224,128]{3,2,1,0:T(8,128)(2,1)} %bitcast.24, ...), custom_call_target="tpu_custom_call" | custom-call | tf_op jit(solution)/shard_map/factor/pallas_call | solution.py:342
  45.6 0.0 copy-start.2
  45.6 1.4 %copy-done.2 = bf16[48,8,16,128]{3,2,1,0:T(8,128)(2,1)S(1)} copy-done((bf16[48,8,16,128]{3,2,1,0:T(8,128)(2,1)S(1)}, bf16[48,8,16,128]{3,2,1,0:T(8,128)(2,1)}, u32[]{:S(2)}) %copy-start.2) | copy-done | bytes 1572888
  47.0 11.7 %halo.1 = (bf16[52,12,16,128]{3,2,1,0:T(8,128)(2,1)S(1)}, bf16[48,8,64,128]{3,2,1,0:T(8,128)(2,1)S(1)}) custom-call(bf16[48,8,16,128]{3,2,1,0:T(8,128)(2,1)S(1)} %copy-done.2), custom_call_target="tpu_custom_call" | custom-call | tf_op jit(solution)/shard_map/halo/pallas_call | solution.py:121
  58.8 0.0 copy-start
  58.8 2.7 %copy-done = bf16[48,8,64,128]{3,2,1,0:T(8,128)(2,1)} copy-done((bf16[48,8,64,128]{3,2,1,0:T(8,128)(2,1)}, bf16[48,8,64,128]{3,2,1,0:T(8,128)(2,1)S(1)}, u32[]{:S(2)}) %copy-start) | copy-done | bytes 6291480
  61.4 0.0 copy-start.1
  61.4 1.4 %copy-done.1 = bf16[52,12,16,128]{3,2,1,0:T(8,128)(2,1)} copy-done((bf16[52,12,16,128]{3,2,1,0:T(8,128)(2,1)}, bf16[52,12,16,128]{3,2,1,0:T(8,128)(2,1)S(1)}, u32[]{:S(2)}) %copy-start.1) | copy-done | bytes 2555928
  62.9 29.9 %apply.1 = f32[48,16,8,128]{3,2,1,0:T(8,128)} custom-call(s32[8,4,48]{2,1,0:T(4,128)} %bitcast.32, f32[48,8,16,128]{3,2,1,0:T(8,128)} %get-tuple-element.15.t_ref, f32[48,8,64]{2,1,0:T(8,128)} %d_ref.1, bf16[48,8,64,128]{3,2,1,0:T(8,128)(2,1)} %copy-done, bf16[52,12,16,128]{3,2,1,0:T(8,128)(2,1)} %copy-done.1, bf16[48,8,32,4,128]{4,3,2,1,0:T(4,128)(2,1)} %bitcast.21), custom_call_target="tpu_custom_call" | custom-call | tf_op jit(solution)/shard_map/apply/pallas_call | solution.py:438
  (4 shorter events, 0.0 us)
Async XLA Ops:
  45.6 1.4 %copy-start.2 = (bf16[48,8,16,128]{3,2,1,0:T(8,128)(2,1)S(1)}, bf16[48,8,16,128]{3,2,1,0:T(8,128)(2,1)}, u32[]{:S(2)}) copy-start(bf16[48,8,16,128]{3,2,1,0:T(8,128)(2,1)} %get-tuple-element.16.src) | copy-start | bytes 4718596
  58.8 2.7 %copy-start = (bf16[48,8,64,128]{3,2,1,0:T(8,128)(2,1)}, bf16[48,8,64,128]{3,2,1,0:T(8,128)(2,1)S(1)}, u32[]{:S(2)}) copy-start(bf16[48,8,64,128]{3,2,1,0:T(8,128)(2,1)S(1)} %get-tuple-element.17.own_ref) | copy-start | bytes 18874372
  61.4 1.4 %copy-start.1 = (bf16[52,12,16,128]{3,2,1,0:T(8,128)(2,1)}, bf16[52,12,16,128]{3,2,1,0:T(8,128)(2,1)S(1)}, u32[]{:S(2)}) copy-start(bf16[52,12,16,128]{3,2,1,0:T(8,128)(2,1)S(1)} %get-tuple-element.18.tp_ref) | copy-start | bytes 7667716

commit v3 on v2

--- a/solution.py
+++ b/solution.py
@@ -122,7 +122,10 @@
         in_specs=[anyspec], out_specs=[anyspec]*2, out_shape=[jax.ShapeDtypeStruct(dst_shape, src.dtype), jax.ShapeDtypeStruct((nx, ny, 64, 128), BF)],
         scratch_shapes=[pltpu.VMEM(src.shape, BF), pltpu.VMEM((nx, ny, 64, 128), BF), pltpu.VMEM((128, 512), BF), pltpu.VMEM((ny, 64, 128), F32),
                         pltpu.SemaphoreType.DMA((1,)), pltpu.SemaphoreType.DMA((4,)), pltpu.SemaphoreType.DMA((8,)), pltpu.SemaphoreType.DMA((8,))],
-        compiler_params=pltpu.CompilerParams(vmem_limit_bytes=40<<20, collective_id=1, has_side_effects=True), name="halo")(src)
+        compiler_params=pltpu.CompilerParams(vmem_limit_bytes=62<<20, collective_id=1, has_side_effects=True), name="halo")(src)
+
+
+UNROLL = 6
 
 
 def pick_blocks(pieces, block):
@@ -132,27 +135,31 @@
     return out
 
 
-def turn(v, s):
-    s = s % 4
-    return v if s == 0 else pltpu.roll(v, 32*s, 1)
-
-
-def gram_rows(x, p_buf, z_buf, g_buf, low_buf, slot):
-    block16 = lax.broadcasted_iota(jnp.int32, (16,128), 1)//32
-    block8 = lax.broadcasted_iota(jnp.int32, (8,128), 1)//32
-    for half in range(2):
-        p = [p_buf[x, 4*half+b] for b in range(4)]
-        yh = jnp.concatenate([pick_blocks([turn(p[b], b-q) for b in range(4)], block16) for q in range(4)], axis=0)
+def transpose_blocks(p, lane):
+    block = lane >> 5
+    return [pick_blocks([p[b] if b == q else pltpu.roll(p[b], 32*((b-q) % 4), 1) for b in range(4)], block) for q in range(4)]
+
+
+def gram_rows(xs, p_buf, z_buf, g_buf, low_buf):
+    lane16 = lax.broadcasted_iota(jnp.int32, (16,128), 1)
+    lane8 = lax.broadcasted_iota(jnp.int32, (8,128), 1)
+    block8 = lane8//32
+    work = [(x, half) for x in xs for half in range(2)]
+    outs = []
+    for x, half in work:
+        yh = jnp.concatenate(transpose_blocks([p_buf[x, 4*half+b] for b in range(4)], lane16), axis=0)
         hi = yh.astype(BF)
         lo = (yh - hi.astype(F32)).astype(BF)
-        o = lax.dot_general(jnp.concatenate([hi, lo, hi], axis=0), jnp.concatenate([hi, hi, lo], axis=0), (((0,),(0,)),((),())), preferred_element_type=F32)
+        outs.append(lax.dot_general(jnp.concatenate([hi, lo, hi], axis=0), jnp.concatenate([hi, hi, lo], axis=0), (((0,),(0,)),((),())), preferred_element_type=F32))
+    for slot, o in enumerate(outs):
         r = [pick_blocks([o[32*b+8*kb:32*b+8*kb+8] for b in range(4)], block8) * (1.0/64) for kb in range(4)]
-        for b in range(4):
-            z_buf[slot, :, b, :] = pick_blocks([turn(r[kb], kb-b) for kb in range(4)], block8)
+        for b, g in enumerate(transpose_blocks(r, lane8)):
+            z_buf[slot, pl.ds(b, 8, stride=4), :] = g
+    for slot, (x, half) in enumerate(work):
         z = z_buf[slot]
         zh = z.astype(BF)
-        g_buf[half, :, x] = zh
-        low_buf[half, :, x] = (z - zh.astype(F32)).astype(BF)
+        g_buf[half, :, x] = zh.reshape(8,4,128)
+        low_buf[half, :, x] = (z - zh.astype(F32)).astype(BF).reshape(8,4,128)
 
 
 def gram_kernel(nx, chunks, with_halo, *refs):
@@ -186,10 +193,9 @@
     for c in range(chunks):
         for one in loads[c]: one.wait()
         def rows(i, carry):
-            for u in range(2):
-                gram_rows(c*part + 2*i + u, p_buf, z_buf, g_buf, low_buf, u)
+            gram_rows([c*part + UNROLL*i + u for u in range(UNROLL)], p_buf, z_buf, g_buf, low_buf)
             return carry
-        lax.fori_loop(0, part//2, rows, 0)
+        lax.fori_loop(0, part//UNROLL, rows, 0)
         if with_halo:
             if c == 0:
                 meet()
@@ -207,17 +213,20 @@
     nx = nn.shape[0]
     anyspec = pl.BlockSpec(memory_space=pl.ANY)
     gshape = jax.ShapeDtypeStruct((4, 8, nx+8, 4, 128), BF)
-    scratch = [pltpu.VMEM((nx,8,16,128),F32), pltpu.VMEM((2,8,4,128),F32), pltpu.VMEM((2,8,nx,4,128),BF), pltpu.VMEM((2,8,nx,4,128),BF),
+    scratch = [pltpu.VMEM((nx,8,16,128),F32), pltpu.VMEM((2*UNROLL,32,128),F32), pltpu.VMEM((2,8,nx,4,128),BF), pltpu.VMEM((2,8,nx,4,128),BF),
                pltpu.SemaphoreType.DMA((chunks,8)), pltpu.SemaphoreType.DMA((3,))]
     lshape = jax.ShapeDtypeStruct((2, 8, nx, 4, 128), BF)
     kern = functools.partial(gram_kernel, nx, chunks, tile is not None)
     if tile is None:
         return pl.pallas_call(kern, in_specs=[anyspec], out_specs=[anyspec]*2, out_shape=[gshape, lshape], scratch_shapes=scratch,
-            compiler_params=pltpu.CompilerParams(vmem_limit_bytes=56<<20), name="gram")(nn)
+            compiler_params=pltpu.CompilerParams(vmem_limit_bytes=62<<20), name="gram")(nn)
     return pl.pallas_call(kern, in_specs=[anyspec]*2, out_specs=[anyspec]*3,
         out_shape=[gshape, lshape, jax.ShapeDtypeStruct((3,3)+tile.shape, tile.dtype)],
         scratch_shapes=scratch + [pltpu.SemaphoreType.DMA((14 + 2*chunks,)), pltpu.SemaphoreType.DMA((14 + 2*chunks,))],
-        compiler_params=pltpu.CompilerParams(vmem_limit_bytes=56<<20, collective_id=0, has_side_effects=True), name="gram")(nn, tile)
+        compiler_params=pltpu.CompilerParams(vmem_limit_bytes=62<<20, collective_id=0, has_side_effects=True), name="gram")(nn, tile)
+
+
+FACTOR_UNROLL = 4
 
 
 def local_slots(nx, ny):
@@ -312,21 +321,23 @@
     for c in loads: c.wait()
     stores = []
     for ch in range(chunks):
-        def one_x(i, c):
-            x = ch*part + i
-            for y in range(8):
+        def rows(i, c):
+            at = [(ch*part + FACTOR_UNROLL*i + u, y) for u in range(FACTOR_UNROLL) for y in range(8)]
+            outs = []
+            for x, y in at:
                 rx, ry = place(root_ref[y, x])
                 r = comp[rx*12 + ry]
                 p = p_buf[x, y]
                 ph = p.astype(BF)
                 plo = (p - ph.astype(F32)).astype(BF)
                 lhs = jnp.concatenate([jnp.concatenate([ph, ph], axis=1), jnp.concatenate([plo, jnp.zeros_like(plo)], axis=1)], axis=0)
-                o = jnp.dot(lhs, bd[r], preferred_element_type=F32)
+                outs.append(jnp.dot(lhs, bd[r], preferred_element_type=F32))
+            for (x, y), o in zip(at, outs):
                 t = o[:16] + o[16:]
                 t_buf[x, y] = t
                 tb_buf[x, y] = t.astype(BF)
             return c
-        lax.fori_loop(0, part, one_x, 0)
+        lax.fori_loop(0, part//FACTOR_UNROLL, rows, 0)
         xs = pl.ds(ch*part, part)
         for c in (pltpu.make_async_copy(t_buf.at[xs], t_ref.at[xs], store.at[0, ch]), pltpu.make_async_copy(tb_buf.at[xs], tb_ref.at[xs], store.at[1, ch])):
             c.start()
@@ -350,7 +361,10 @@
         compiler_params=pltpu.CompilerParams(vmem_limit_bytes=62<<20), name="factor")(cells, roots, rid, nn, gpad, glow)
 
 
-def apply_kernel(nx, px, py, xb, idx_ref, t_ref, d_ref, own_ref, tp_ref, a_ref, out_ref, abuf, table, wide, tall, fan_ref, scale_ref, tbuf, obuf, sems, osem, tsem):
+APPLY_UNROLL = 4
+
+
+def apply_kernel(nx, px, py, xb, idx_ref, t_ref, d_ref, own_ref, tp_ref, a_ref, out_ref, abuf, table, wide, tall, fan_ref, pick_ref, scale_ref, tbuf, obuf, sems, osem, tsem):
     step = pl.program_id(0)
     steps = nx // xb
     slot = lax.rem(step, 2)
@@ -374,6 +388,7 @@
         own.start()
         fetch(0, 0)
         fan_ref[...] = spread_lanes()
+        pick_ref[...] = jnp.where((lax.broadcasted_iota(jnp.int32, (128, 128), 0) & 3) == lax.broadcasted_iota(jnp.int32, (128, 128), 1) >> 5, 1.0, 0.0).astype(BF)
         for c in fill: c.wait()
         def ends(i, carry):
             x = jnp.where(i < 2, i, px - 4 + i)
@@ -396,36 +411,37 @@
     def _():
         for c in outs(step-2, slot): c.wait()
     pltpu.make_async_copy(abuf.at[slot], abuf.at[slot], sems.at[slot]).wait()
-    row16 = lax.broadcasted_iota(jnp.int32, (16, 128), 0)
-    col4 = (lax.broadcasted_iota(jnp.int32, (16, 128), 1) % 64) // 4
-    pick = (lax.broadcasted_iota(jnp.int32, (64, 128), 0) % 4 == lax.broadcasted_iota(jnp.int32, (64, 128), 1) // 32)
-    pick = jnp.where(pick, 1.0, 0.0).astype(BF)
-    pick = jnp.concatenate([pick, pick], axis=0)
+    diagonal = (lax.broadcasted_iota(jnp.int32, (16, 128), 1) & 63) >> 2 == lax.broadcasted_iota(jnp.int32, (16, 128), 0)
     lanew = lax.broadcasted_iota(jnp.int32, (64, 128), 1)
-    def one_x(xi, carry):
-        d = d_ref[xi] * OMEGA
-        hi = d.astype(BF).astype(F32)
-        both = jnp.concatenate([hi, d - hi], axis=1)
-        spread = jnp.concatenate([jnp.where(row16 == col4, both[y:y+1], 0.0) for y in range(8)], axis=0)
-        scale_ref[...] = jnp.dot(spread.astype(BF), pick, preferred_element_type=F32)
-        for y in range(8):
-            x = step*xb + xi
-            parts = []
-            for kp in range(2):
-                t0 = load_at(idx_ref[y, 2*kp, x])
-                t1 = load_at(idx_ref[y, 2*kp+1, x])
-                r = jnp.where(lanew < 64, t0, t1)
-                parts.append(jnp.where((lanew//32) % 2 == 0, r, jnp.zeros_like(r)))
-                parts.append(jnp.where((lanew//32) % 2 == 1, r, jnp.zeros_like(r)))
-            rhs = jnp.concatenate(parts, axis=0)
-            lhs = jnp.concatenate([abuf[slot, xi, y, 0], abuf[slot, xi, y, 1]], axis=1)
-            wide[y] = jnp.dot(lhs, rhs, preferred_element_type=F32)
-        for y in range(8):
-            r = [[wide[y, pl.ds(32*ch+p, 16, stride=2), :] for p in range(2)] for ch in range(2)]
-            u = jnp.where(lane < 64, r[0][0], r[1][1]) + pltpu.roll(jnp.where(lane < 64, r[1][0], r[0][1]), 64, 1)
-            obuf[slot, xi, y] = t_ref[xi, y] - scale_ref[16*y:16*y+16, :] * u
+    even = (lanew & 32) == 0
+    left = lanew < 64
+    zero = jnp.zeros((64, 128), BF)
+    def some_rows(i, carry):
+        xis = [APPLY_UNROLL*i + u for u in range(APPLY_UNROLL)]
+        for u, xi in enumerate(xis):
+            d = d_ref[xi] * OMEGA
+            hi = d.astype(BF).astype(F32)
+            both = jnp.concatenate([hi, d - hi], axis=1)
+            spread = jnp.concatenate([jnp.where(diagonal, both[y:y+1], 0.0) for y in range(8)], axis=0)
+            scale_ref[u] = jnp.dot(spread.astype(BF), pick_ref[...], preferred_element_type=F32)
+        for u, xi in enumerate(xis):
+            for y in range(8):
+                x = step*xb + xi
+                parts = []
+                for kp in range(2):
+                    r = jnp.where(left, load_at(idx_ref[y, 2*kp, x]), load_at(idx_ref[y, 2*kp+1, x]))
+                    parts.append(jnp.where(even, r, zero))
+                    parts.append(jnp.where(even, zero, r))
+                rhs = jnp.concatenate(parts, axis=0)
+                lhs = jnp.concatenate([abuf[slot, xi, y, 0], abuf[slot, xi, y, 1]], axis=1)
+                wide[u, y] = jnp.dot(lhs, rhs, preferred_element_type=F32)
+        for u, xi in enumerate(xis):
+            for y in range(8):
+                r = [[wide[u, y, pl.ds(32*ch+p, 16, stride=2), :] for p in range(2)] for ch in range(2)]
+                v = jnp.where(lane < 64, r[0][0], r[1][1]) + pltpu.roll(jnp.where(lane < 64, r[1][0], r[0][1]), 64, 1)
+                obuf[slot, xi, y] = t_ref[xi, y] - scale_ref[u, 16*y:16*y+16, :] * v
         return carry
-    lax.fori_loop(0, xb, one_x, 0)
+    lax.fori_loop(0, xb//APPLY_UNROLL, some_rows, 0)
     for c in outs(step, slot): c.start()
     @pl.when(step == steps - 1)
     def _():
@@ -440,10 +456,10 @@
           in_specs=[pl.BlockSpec((xb,8,16,128), lambda i,*_:(i,0,0,0)), pl.BlockSpec((xb,8,64), lambda i,*_:(i,0,0)),
                     anyspec, anyspec, anyspec],
           out_specs=anyspec,
-          scratch_shapes=[pltpu.VMEM((2,xb,8,2,64,128),BF), pltpu.VMEM((px,py,64,128),BF), pltpu.VMEM((8,64,128),F32), pltpu.VMEM((12,64,128),F32), pltpu.VMEM((128,512),BF), pltpu.VMEM((128,128),F32),
+          scratch_shapes=[pltpu.VMEM((2,xb,8,2,64,128),BF), pltpu.VMEM((px,py,64,128),BF), pltpu.VMEM((APPLY_UNROLL,8,64,128),F32), pltpu.VMEM((12,64,128),F32), pltpu.VMEM((128,512),BF), pltpu.VMEM((128,128),BF), pltpu.VMEM((APPLY_UNROLL,128,128),F32),
              pltpu.VMEM((px,py,16,128),BF), pltpu.VMEM((2,xb,8,16,128),F32), pltpu.SemaphoreType.DMA((2,)), pltpu.SemaphoreType.DMA((2,8)), pltpu.SemaphoreType.DMA((5,))]),
         out_shape=jax.ShapeDtypeStruct((nx,16,8,128),F32),
-        compiler_params=pltpu.CompilerParams(vmem_limit_bytes=56<<20), name="apply")(idx, t4, d, own, tp, a6)
+        compiler_params=pltpu.CompilerParams(vmem_limit_bytes=62<<20), name="apply")(idx, t4, d, own, tp, a6)
 
 
 def body(near_null, a_blocks, inv_diag, root_map, neighbours):

time: 93.4 us -> 69.5 us (0.74)
  Pallas kernels: 83.5 us -> 65.1 us
  local copies, waits for them, and re-layouts: 8.43 us -> 2.94 us
    pallas_call x1, Pallas kernels: 29.9 us -> 20.3 us  [apply_call(): pl.pallas_call(functools.partial(apply_kernel, nx, px, py, xb), grid_spec...]
    unnamed x6 -> x0, local copies, waits for them, and re-layouts: 5.51 us -> none
    pallas_call x1, Pallas kernels: 20.3 us -> 15.3 us  [factor_call(): pl.pallas_call(functools.partial(factor_kernel, nx), grid_spec=pltpu.Pref...]
    pallas_call x1, Pallas kernels: 21.6 us -> 17.3 us  [gram_call(): pl.pallas_call(kern, in_specs=[anyspec] * 2, out_specs=[anyspec] * 3, out...]
where the time goes in v3:
time: 69.5 us; the launch traced here: 68.9 us
  Pallas kernels  65.1 us (94%)
  local copies, waits for them, and re-layouts  2.94 us (4%)
  other arithmetic  0.78 us (1%)
    pallas_call x1, Pallas kernels, apply_call(): pl.pallas_call(functools.partial(apply_kernel, nx, px, py, xb), grid_spec...  20.3 us
    pallas_call x1, Pallas kernels, gram_call(): pl.pallas_call(kern, in_specs=[anyspec] * 2, out_specs=[anyspec] * 3, out...  17.3 us
    pallas_call x1, Pallas kernels, factor_call(): pl.pallas_call(functools.partial(factor_kernel, nx), grid_spec=pltpu.Pref...  15.3 us
    pallas_call x1, Pallas kernels, halo_call(): pl.pallas_call(functools.partial(halo_kernel, nx, ny, width), in_specs=[a...  12.2 us

profile of v3, /device:TPU:7, one launch (start us, length us, event | category | flops | bytes accessed | tf_op | source)
XLA Modules:
  0.0 68.9 jit_solution(14721805610053038748)
XLA Ops:
  0.0 0.1 slice.9
  0.1 0.1 slice.10
  0.2 0.8 %copy.10 = s32[48,2,4]{2,0,1:T(8,128)S(1)} copy(s32[48,2,4]{0,2,1:T(4,128)} %bitcast.29) | data formatting | bytes 3072 | tf_op jit(solution)/shard_map/reshape | solution.py:479
  1.0 0.1 reshape.64
  1.1 17.3 %gram.1 = (bf16[4,8,56,4,128]{4,3,2,1,0:T(4,128)(2,1)}, bf16[2,8,48,4,128]{4,3,2,1,0:T(4,128)(2,1)}, s32[3,3,8,48]{3,2,1,0:T(8,128)}) custom-call(f32[48,16,8,128]{3,2,1,0:T(8,128)} %bitcast.22, s32[8,48]{1,0:T(8,128)} %bitcast.30), custom_call_target="tpu_custom_call" | custom-call | tf_op jit(solution)/shard_map/gram/pallas_call | solution.py:223
  18.4 0.8 %copy.7 = s32[3,48,3,8]{1,0,3,2:T(4,128)S(1)} copy(s32[3,48,3,8]{1,3,2,0:T(8,128)} %bitcast.28) | data formatting | bytes 27648 | tf_op jit(solution)/shard_map/transpose | solution.py:474
  19.2 0.1 reshape.59
  19.2 0.1 slice_select_fusion
  19.3 0.1 compare_select_fusion
  19.4 0.1 copy.8
  19.5 0.7 %reshape.60.cells_ref = s32[624]{0:T(1024)} reshape(s32[52,12]{1,0:T(8,128)S(1)} %copy.8) | data formatting | bytes 4992 | tf_op jit(solution)/shard_map/reshape | solution.py:478
  20.2 0.1 copy.9
  20.3 0.1 reshape.62
  20.4 0.6 pad_add_fusion.rid_ref
  21.0 15.3 %factor.1 = (f32[48,8,16,128]{3,2,1,0:T(8,128)}, bf16[48,8,16,128]{3,2,1,0:T(8,128)(2,1)}) custom-call(s32[624]{0:T(1024)} %reshape.60.cells_ref, s32[8,48]{1,0:T(8,128)} %bitcast.31, s32[1,1280]{1,0:T(1,128)} %pad_add_fusion.rid_ref, f32[48,16,8,128]{3,2,1,0:T(8,128)} %bitcast.23, bf16[4,8,224,128]{3,2,1,0:T(8,128)(2,1)} %bitcast.24, ...), custom_call_target="tpu_custom_call" | custom-call | tf_op jit(solution)/shard_map/factor/pallas_call | solution.py:353
  36.4 12.2 %halo.1 = (bf16[52,12,16,128]{3,2,1,0:T(8,128)(2,1)}, bf16[48,8,64,128]{3,2,1,0:T(8,128)(2,1)}) custom-call(bf16[48,8,16,128]{3,2,1,0:T(8,128)(2,1)} %get-tuple-element.16.src), custom_call_target="tpu_custom_call" | custom-call | tf_op jit(solution)/shard_map/halo/pallas_call | solution.py:121
  48.6 20.3 %apply.1 = f32[48,16,8,128]{3,2,1,0:T(8,128)} custom-call(s32[8,4,48]{2,1,0:T(4,128)} %bitcast.32, f32[48,8,16,128]{3,2,1,0:T(8,128)} %get-tuple-element.15.t_ref, f32[48,8,64]{2,1,0:T(8,128)} %d_ref.1, bf16[48,8,64,128]{3,2,1,0:T(8,128)(2,1)} %get-tuple-element.17.own_ref, bf16[52,12,16,128]{3,2,1,0:T(8,128)(2,1)} %get-tuple-element.18.tp_ref, ...), custom_call_target="tpu_custom_call" | custom-call | tf_op jit(solution)/shard_map/apply/pallas_call | solution.py:454
  (4 shorter events, 0.0 us)

commit v4 on v3

--- a/solution.py
+++ b/solution.py
@@ -102,11 +102,12 @@
     stores = []
     for c in range(chunks):
         def expand(i, carry):
-            x = c*part + i
-            for y, t in enumerate(expanded(buf[x].reshape(ny*16, 128), fan_ref, tall)):
-                table[x, y] = t
+            x = c*part + 3*i
+            rows = jnp.concatenate([buf[x+u].reshape(ny*16, 128) for u in range(3)], axis=0)
+            for e, t in enumerate(expanded(rows, fan_ref, tall)):
+                table[x + e//ny, e % ny] = t
             return carry
-        lax.fori_loop(0, part, expand, 0)
+        lax.fori_loop(0, part//3, expand, 0)
         xs = pl.ds(c*part, part)
         stores.append(pltpu.make_async_copy(table.at[xs], own_table.at[xs], store.at[c]))
         stores[-1].start()
@@ -120,7 +121,7 @@
     nx, ny = src.shape[:2]
     return pl.pallas_call(functools.partial(halo_kernel, nx, ny, width),
         in_specs=[anyspec], out_specs=[anyspec]*2, out_shape=[jax.ShapeDtypeStruct(dst_shape, src.dtype), jax.ShapeDtypeStruct((nx, ny, 64, 128), BF)],
-        scratch_shapes=[pltpu.VMEM(src.shape, BF), pltpu.VMEM((nx, ny, 64, 128), BF), pltpu.VMEM((128, 512), BF), pltpu.VMEM((ny, 64, 128), F32),
+        scratch_shapes=[pltpu.VMEM(src.shape, BF), pltpu.VMEM((nx, ny, 64, 128), BF), pltpu.VMEM((128, 512), BF), pltpu.VMEM((3*ny, 64, 128), F32),
                         pltpu.SemaphoreType.DMA((1,)), pltpu.SemaphoreType.DMA((4,)), pltpu.SemaphoreType.DMA((8,)), pltpu.SemaphoreType.DMA((8,))],
         compiler_params=pltpu.CompilerParams(vmem_limit_bytes=62<<20, collective_id=1, has_side_effects=True), name="halo")(src)
 
@@ -361,7 +362,7 @@
         compiler_params=pltpu.CompilerParams(vmem_limit_bytes=62<<20), name="factor")(cells, roots, rid, nn, gpad, glow)
 
 
-APPLY_UNROLL = 4
+APPLY_UNROLL = 6
 
 
 def apply_kernel(nx, px, py, xb, idx_ref, t_ref, d_ref, own_ref, tp_ref, a_ref, out_ref, abuf, table, wide, tall, fan_ref, pick_ref, scale_ref, tbuf, obuf, sems, osem, tsem):
@@ -391,18 +392,19 @@
         pick_ref[...] = jnp.where((lax.broadcasted_iota(jnp.int32, (128, 128), 0) & 3) == lax.broadcasted_iota(jnp.int32, (128, 128), 1) >> 5, 1.0, 0.0).astype(BF)
         for c in fill: c.wait()
         def ends(i, carry):
-            x = jnp.where(i < 2, i, px - 4 + i)
-            for y, t in enumerate(expanded(tbuf[x].reshape(py*16, 128), fan_ref, tall)):
-                table[x, y] = t
+            x = i*(px - 2)
+            rows = jnp.concatenate([tbuf[x+u].reshape(py*16, 128) for u in range(2)], axis=0)
+            for e, t in enumerate(expanded(rows, fan_ref, tall)):
+                table[x + e//py, e % py] = t
             return carry
-        lax.fori_loop(0, 4, ends, 0)
+        lax.fori_loop(0, 2, ends, 0)
         def sides(i, carry):
-            at = [(2 + 3*i + u, y) for u in range(3) for y in (0, 1, py-2, py-1)]
+            at = [(2 + 6*i + u, y) for u in range(6) for y in (0, 1, py-2, py-1)]
             rows = jnp.concatenate([tbuf[x, y] for x, y in at], axis=0)
             for (x, y), t in zip(at, expanded(rows, fan_ref, tall)):
                 table[x, y] = t
             return carry
-        lax.fori_loop(0, nx//3, sides, 0)
+        lax.fori_loop(0, nx//6, sides, 0)
         own.wait()
     @pl.when(step + 1 < steps)
     def _():
@@ -456,7 +458,7 @@
           in_specs=[pl.BlockSpec((xb,8,16,128), lambda i,*_:(i,0,0,0)), pl.BlockSpec((xb,8,64), lambda i,*_:(i,0,0)),
                     anyspec, anyspec, anyspec],
           out_specs=anyspec,
-          scratch_shapes=[pltpu.VMEM((2,xb,8,2,64,128),BF), pltpu.VMEM((px,py,64,128),BF), pltpu.VMEM((APPLY_UNROLL,8,64,128),F32), pltpu.VMEM((12,64,128),F32), pltpu.VMEM((128,512),BF), pltpu.VMEM((128,128),BF), pltpu.VMEM((APPLY_UNROLL,128,128),F32),
+          scratch_shapes=[pltpu.VMEM((2,xb,8,2,64,128),BF), pltpu.VMEM((px,py,64,128),BF), pltpu.VMEM((APPLY_UNROLL,8,64,128),F32), pltpu.VMEM((24,64,128),F32), pltpu.VMEM((128,512),BF), pltpu.VMEM((128,128),BF), pltpu.VMEM((APPLY_UNROLL,128,128),F32),
              pltpu.VMEM((px,py,16,128),BF), pltpu.VMEM((2,xb,8,16,128),F32), pltpu.SemaphoreType.DMA((2,)), pltpu.SemaphoreType.DMA((2,8)), pltpu.SemaphoreType.DMA((5,))]),
         out_shape=jax.ShapeDtypeStruct((nx,16,8,128),F32),
         compiler_params=pltpu.CompilerParams(vmem_limit_bytes=62<<20), name="apply")(idx, t4, d, own, tp, a6)

time: 69.5 us -> 64.4 us (0.927)
  Pallas kernels: 65.1 us -> 60.1 us
    pallas_call x1, Pallas kernels: 12.2 us -> 9.63 us  [halo_call(): pl.pallas_call(functools.partial(halo_kernel, nx, ny, width), in_specs=[a...]
    pallas_call x1, Pallas kernels: 20.3 us -> 18.1 us  [apply_call(): pl.pallas_call(functools.partial(apply_kernel, nx, px, py, xb), grid_spec...]
where the time goes in v4:
time: 64.4 us; the launch traced here: 63.8 us
  Pallas kernels  60.1 us (93%)
  local copies, waits for them, and re-layouts  2.94 us (5%)
  other arithmetic  0.78 us (1%)
    pallas_call x1, Pallas kernels, apply_call(): pl.pallas_call(functools.partial(apply_kernel, nx, px, py, xb), grid_spec...  18.1 us
    pallas_call x1, Pallas kernels, gram_call(): pl.pallas_call(kern, in_specs=[anyspec] * 2, out_specs=[anyspec] * 3, out...  17.3 us
    pallas_call x1, Pallas kernels, factor_call(): pl.pallas_call(functools.partial(factor_kernel, nx), grid_spec=pltpu.Pref...  15.1 us
    pallas_call x1, Pallas kernels, halo_call(): pl.pallas_call(functools.partial(halo_kernel, nx, ny, width), in_specs=[a...  9.63 us

profile of v4, /device:TPU:7, one launch (start us, length us, event | category | flops | bytes accessed | tf_op | source)
XLA Modules:
  0.0 63.8 jit_solution(14557893421018034203)
XLA Ops:
  0.0 0.1 slice.9
  0.1 0.1 slice.10
  0.2 0.8 %copy.10 = s32[48,2,4]{2,0,1:T(8,128)S(1)} copy(s32[48,2,4]{0,2,1:T(4,128)} %bitcast.29) | data formatting | bytes 3072 | tf_op jit(solution)/shard_map/reshape | solution.py:481
  1.0 0.1 reshape.64
  1.1 17.3 %gram.1 = (bf16[4,8,56,4,128]{4,3,2,1,0:T(4,128)(2,1)}, bf16[2,8,48,4,128]{4,3,2,1,0:T(4,128)(2,1)}, s32[3,3,8,48]{3,2,1,0:T(8,128)}) custom-call(f32[48,16,8,128]{3,2,1,0:T(8,128)} %bitcast.22, s32[8,48]{1,0:T(8,128)} %bitcast.30), custom_call_target="tpu_custom_call" | custom-call | tf_op jit(solution)/shard_map/gram/pallas_call | solution.py:224
  18.4 0.8 %copy.7 = s32[3,48,3,8]{1,0,3,2:T(4,128)S(1)} copy(s32[3,48,3,8]{1,3,2,0:T(8,128)} %bitcast.28) | data formatting | bytes 27648 | tf_op jit(solution)/shard_map/transpose | solution.py:476
  19.2 0.1 reshape.59
  19.2 0.1 slice_select_fusion
  19.3 0.1 compare_select_fusion
  19.4 0.1 copy.8
  19.5 0.7 %reshape.60.cells_ref = s32[624]{0:T(1024)} reshape(s32[52,12]{1,0:T(8,128)S(1)} %copy.8) | data formatting | bytes 4992 | tf_op jit(solution)/shard_map/reshape | solution.py:480
  20.2 0.1 copy.9
  20.3 0.1 reshape.62
  20.4 0.6 pad_add_fusion.rid_ref
  21.0 15.1 %factor.1 = (f32[48,8,16,128]{3,2,1,0:T(8,128)}, bf16[48,8,16,128]{3,2,1,0:T(8,128)(2,1)}) custom-call(s32[624]{0:T(1024)} %reshape.60.cells_ref, s32[8,48]{1,0:T(8,128)} %bitcast.31, s32[1,1280]{1,0:T(1,128)} %pad_add_fusion.rid_ref, f32[48,16,8,128]{3,2,1,0:T(8,128)} %bitcast.23, bf16[4,8,224,128]{3,2,1,0:T(8,128)(2,1)} %bitcast.24, ...), custom_call_target="tpu_custom_call" | custom-call | tf_op jit(solution)/shard_map/factor/pallas_call | solution.py:354
  36.1 9.6 %halo.1 = (bf16[52,12,16,128]{3,2,1,0:T(8,128)(2,1)}, bf16[48,8,64,128]{3,2,1,0:T(8,128)(2,1)}) custom-call(bf16[48,8,16,128]{3,2,1,0:T(8,128)(2,1)} %get-tuple-element.16.src), custom_call_target="tpu_custom_call" | custom-call | tf_op jit(solution)/shard_map/halo/pallas_call | solution.py:122
  45.7 18.1 %apply.1 = f32[48,16,8,128]{3,2,1,0:T(8,128)} custom-call(s32[8,4,48]{2,1,0:T(4,128)} %bitcast.32, f32[48,8,16,128]{3,2,1,0:T(8,128)} %get-tuple-element.15.t_ref, f32[48,8,64]{2,1,0:T(8,128)} %d_ref.1, bf16[48,8,64,128]{3,2,1,0:T(8,128)(2,1)} %get-tuple-element.17.own_ref, bf16[52,12,16,128]{3,2,1,0:T(8,128)(2,1)} %get-tuple-element.18.tp_ref, ...), custom_call_target="tpu_custom_call" | custom-call | tf_op jit(solution)/shard_map/apply/pallas_call | solution.py:456
  (4 shorter events, 0.0 us)
